TPU v7x, 512 devices: a whole 4x4x16 slice. The times are simulated.
512 devices in a mesh: tm: 16 (over y_hi, x, core), space: 32 (over z, y_lo).
Axes of the slice: x: 4, y: 4 (y_hi: 2, y_lo: 2; y = y_hi * 2 + y_lo), z: 16, core: 2. Of those that a mesh axis runs over, the one named last changes fastest.
Arguments:
- start_states: float32 [16, 512, 1024], P('tm', 'space'), may hold values from -6 to 6
- sigma: float32 [512, 1024], P('space'), may hold values from 0.05 to 5
- labels: int32 [512, 1024], P('space'), may hold values from 0 to 3
- nu_table: float32 [4], replicated, may hold values from 0.3 to 3
- coil: float32 [512, 1024], P('space'), may hold values from -6 to 6
- waveform: float32 [256], P('tm'), may hold values from -4 to 4
Outputs:
- end_states: float32 [16, 512, 1024], P('tm', 'space')
- traces_out: float32 [256, 32768], P('tm', 'space')
All inputs are finite; a program needn't handle non-finite values.
Results may differ from a plain program's by a relative error of at most 0.000026.
Values sent between devices are 32-bit elements; how exact they have to be, the bound alone decides.
A program may use at most 64 MiB of HBM per device.

v0:
```python
import jax
import jax.numpy as jnp
from jax import lax
from jax.sharding import PartitionSpec as P

JACOBI = 8
SWEEPS = 2


THETA = 0.25


def passed_along(array, axis, by):
    peers = lax.axis_size(axis)
    pairs = [(i, i + by) for i in range(peers) if 0 <= i + by < peers]
    return lax.ppermute(array, axis, pairs)


def from_behind(value, axis, steps):
    count = lax.axis_size(axis)
    pairs = [(source, (source + steps) % count) for source in range(count)]
    return lax.ppermute(value, axis, pairs)


def shifted(field, axis, low, high):
    config = [(0, 0, 0)] * field.ndim
    config[axis % field.ndim] = (low, high, 0)
    return lax.pad(field, jnp.zeros((), field.dtype), config)


def next_column(field):
    return shifted(field, -2, -1, 1)


def prev_column(field):
    return shifted(field, -2, 1, -1)


def next_row(field):
    return shifted(field, -1, -1, 1)


def prev_row(field):
    return shifted(field, -1, 1, -1)


def harmonic(first_nu, second_nu):
    return 2.0 * first_nu * second_nu / (first_nu + second_nu)


def reluctivity(labels, nu_table):
    result = jnp.zeros(labels.shape, jnp.float32)
    for material in range(nu_table.shape[0]):
        result = result + jnp.where(labels == material, nu_table[material], jnp.float32(0.0))
    return result


def coefficients(sigma, nu, first, last):
    kxp = harmonic(nu, next_column(nu))
    kxm = harmonic(nu, prev_column(nu))
    kyp = harmonic(nu, next_row(nu))
    kym = harmonic(nu, prev_row(nu))
    rows = jnp.arange(nu.shape[-1])
    edge_rows = ((rows == 0) | (rows == nu.shape[-1] - 1)).astype(jnp.float32)
    inner = sigma + kxp + kxm + kyp + kym + 2.0 * nu * edge_rows
    left_coef = 2.0 * nu[..., 0, :]
    right_coef = 2.0 * nu[..., -1, :]
    cols = jnp.arange(nu.shape[-2])[:, None]
    at_left = (cols == 0).astype(jnp.float32)
    at_right = (cols == nu.shape[-2] - 1).astype(jnp.float32)
    d_dir = inner + at_left * left_coef[..., None, :] + at_right * right_coef[..., None, :]
    d_neu = (
        inner
        + at_left * (first * left_coef)[..., None, :]
        + at_right * (last * right_coef)[..., None, :]
    )
    return ((sigma, kxp, kxm, kyp, kym), left_coef, right_coef, d_dir, d_neu)


def march(start, couple, diag, coil, waves, left_term, right_term):
    sigma, kxp, kxm, kyp, kym = couple
    cols = jnp.arange(start.shape[-2])[:, None]
    at_left = (cols == 0).astype(jnp.float32)
    at_right = (cols == start.shape[-2] - 1).astype(jnp.float32)

    def advance(previous, inputs):
        wave, left_val, right_val = inputs
        rhs = (
            sigma * previous
            + coil * wave
            + at_left * left_val[..., None, :]
            + at_right * right_val[..., None, :]
        )
        field = previous
        for repeat in range(JACOBI):
            total = (
                rhs
                + kxp * next_column(field)
                + kxm * prev_column(field)
                + kyp * next_row(field)
                + kym * prev_row(field)
            )
            field = total / diag
        return (field, (field[..., 0, :], field[..., -1, :]))

    return lax.scan(advance, start, (waves, left_term, right_term))


def body(start_states, sigma, labels, nu_table, coil, waveform):
    states = start_states[0]
    nu = reluctivity(labels, nu_table)
    place = lax.axis_index("space")
    count = lax.axis_size("space")
    first = (place == 0).astype(jnp.float32)
    last = (place == count - 1).astype(jnp.float32)
    couple, left_coef, right_coef, d_dir, d_neu = coefficients(sigma, nu, first, last)
    zero_waves = jnp.zeros_like(waveform)
    traces = jnp.zeros((waveform.shape[0], states.shape[1]), jnp.float32)
    left_traces = jnp.zeros_like(traces)
    inner_face = 1.0 - last
    ends = states
    for relax_round in range(SWEEPS):
        if relax_round > 0:
            left_traces = passed_along(traces, "space", 1)
        left_term = left_coef * left_traces
        right_term = right_coef * traces
        ends, (firsts, lasts) = march(states, couple, d_dir, coil, waveform, left_term, right_term)
        nb_first, nb_coef = passed_along((firsts, left_coef), "space", -1)
        flux = inner_face * (right_coef * (lasts - traces) + nb_coef * (nb_first - traces))
        flux_left = passed_along(flux, "space", 1)
        unused, (pfirst, plast) = march(
            jnp.zeros_like(states), couple, d_neu, coil, zero_waves, flux_left, flux
        )
        nb_pfirst = passed_along(pfirst, "space", -1)
        traces = traces + THETA * inner_face * (plast + nb_pfirst)
        if relax_round + 1 < SWEEPS:
            states = from_behind(ends, "tm", 1)
    return (ends[None], traces)


def solution(mesh):
    placed = (
        P("tm", "space", None),
        P("space", None),
        P("space", None),
        P(),
        P("space", None),
        P("tm"),
    )
    return jax.shard_map(
        body,
        mesh=mesh,
        in_specs=placed,
        out_specs=(P("tm", "space", None), P("tm", "space")),
        check_vma=False,
    )
```

profile of v0, /device:TPU:120, one launch (start us, length us, event | category | flops | bytes accessed | tf_op | source)
XLA Modules:
  0.0 183.3 jit_solution(10971371566611396437)
XLA Ops:
  2.0 2.6 %select_add_fusion = f32[16,1024]{1,0:T(8,128)S(1)} fusion(s32[16,1024]{1,0:T(8,128)S(1)} %copy-done.3, f32[]{:T(128)} %bitcast.4, f32[]{:T(128)} %bitcast.3, f32[]{:T(128)} %bitcast.2, f32[]{:T(128)} %bitcast.1), kind=kLoop, calls=%fused_computation.469 | loop fusion | flops 180224 | bytes 131088 | tf_op jit(solution)/shard_map/add | solution.py:54
  5.0 0.8 copy-done.1
  5.8 38.7 %while.60 = (s32[]{:T(128)}, f32[16,1024]{1,0:T(8,128)S(1)}, f32[16,1024]{1,0:T(8,128)S(1)}, f32[16,1024]{1,0:T(8,128)S(1)}, f32[16,1024]{1,0:T(8,128)S(1)}, /*i...) while((s32[]{:T(128)}, f32[16,1024]{1,0:T(8,128)S(1)}, ...), condition=%wide.region_1.2_spmd.clone, body=%wide.region_0.1_spmd.clone.sunk | while | flops 1294402 | bytes 4383153 | solution.py:106
  11.2 0.7 fusion.360
  13.7 0.7 fusion.360
  16.1 0.7 fusion.360
  18.5 0.7 fusion.360
  20.9 0.7 fusion.360
  23.3 0.7 fusion.360
  25.8 0.7 fusion.360
  28.2 0.7 fusion.360
  30.6 0.7 fusion.360
  44.5 2.7 %collective-permute-start.2 = (f32[16,1024]{1,0:T(8,128)S(1)}, f32[16,1024]{1,0:T(8,128)S(1)}, u32[]{:S(2)}, u32[]{:S(2)}) collective-permute-start(f32[16,1024]{1,0:T(8,128)S(1)} %get-tuple-element.328), channel_id=1, source_target_pairs={{1,0},{2,1},{3,2},{4,3},{5,4},{6,5},{7,6},{8,7},{9,8},{10,9},{11,1... | collective-permute-start | bytes 196616 | tf_op jit(solution)/shard_map/ppermute | solution.py:16
  47.2 2.7 %collective-permute-start.1 = (f32[1024]{0:T(1024)S(1)}, f32[1024]{0:T(1024)S(1)}, u32[]{:S(2)}, u32[]{:S(2)}) collective-permute-start(f32[1024]{0:T(1024)S(1)} %bitcast.81), channel_id=1, source_target_pairs={{1,0},{2,1},{3,2},{4,3},{5,4},{6,5},{7,6},{8,7},{9,8},{10,9},{11,1... | collective-permute-start | bytes 12296 | tf_op jit(solution)/shard_map/ppermute | solution.py:16
  49.9 4.9 %collective-permute-done.1 = f32[1024]{0:T(1024)S(1)} collective-permute-done((f32[1024]{0:T(1024)S(1)}, f32[1024]{0:T(1024)S(1)}, u32[]{:S(2)}, u32[]{:S(2)}) %collective-permute-start.1) | collective-permute-done | bytes 4128 | tf_op jit(solution)/shard_map/ppermute | solution.py:16
  54.8 3.2 %collective-permute-start.3 = (f32[16,1024]{1,0:T(8,128)S(1)}, f32[16,1024]{1,0:T(8,128)S(1)}, u32[]{:S(2)}, u32[]{:S(2)}) collective-permute-start(f32[16,1024]{1,0:T(8,128)S(1)} %add_multiply_fusion.2), channel_id=1, source_target_pairs={{0,1},{1,2},{2,3},{3,4},{4,5},{5,6},{6,7},{7,8},{8,9},{9,10},{10,1... | collective-permute-start | bytes 196616 | tf_op jit(solution)/shard_map/ppermute | solution.py:16
  58.0 3.0 %collective-permute-done.3 = f32[16,1024]{1,0:T(8,128)S(1)} collective-permute-done((f32[16,1024]{1,0:T(8,128)S(1)}, f32[16,1024]{1,0:T(8,128)S(1)}, u32[]{:S(2)}, u32[]{:S(2)}) %collective-permute-start.3) | collective-permute-done | bytes 65568 | tf_op jit(solution)/shard_map/ppermute | solution.py:16
  61.0 19.5 %while.62 = (s32[]{:T(128)}, f32[16,1024]{1,0:T(8,128)S(1)}, f32[16,1024]{1,0:T(8,128)S(1)}, f32[16,1024]{1,0:T(8,128)S(1)}, f32[16,1024]{1,0:T(8,128)S(1)}, /*i...) while((s32[]{:T(128)}, f32[16,1024]{1,0:T(8,128)S(1)}, ...), condition=%wide.region_3.4_spmd.clone, body=%wide.region_2.3_spmd.clone.sunk | while | flops 1310787 | bytes 4514211 | solution.py:106
  80.5 1.9 %collective-permute-start.4 = (f32[16,1024]{1,0:T(8,128)S(1)}, f32[16,1024]{1,0:T(8,128)S(1)}, u32[]{:S(2)}, u32[]{:S(2)}) collective-permute-start(f32[16,1024]{1,0:T(8,128)S(1)} %get-tuple-element.330), channel_id=1, source_target_pairs={{1,0},{2,1},{3,2},{4,3},{5,4},{6,5},{7,6},{8,7},{9,8},{10,9},{11,1... | collective-permute-start | bytes 196616 | tf_op jit(solution)/shard_map/ppermute | solution.py:16
  82.4 6.3 %collective-permute-done.4 = f32[16,1024]{1,0:T(8,128)S(1)} collective-permute-done((f32[16,1024]{1,0:T(8,128)S(1)}, f32[16,1024]{1,0:T(8,128)S(1)}, u32[]{:S(2)}, u32[]{:S(2)}) %collective-permute-start.4) | collective-permute-done | bytes 65568 | tf_op jit(solution)/shard_map/ppermute | solution.py:16
  88.8 3.2 %collective-permute-start.5 = (f32[16,1024]{1,0:T(8,128)S(1)}, f32[16,1024]{1,0:T(8,128)S(1)}, u32[]{:S(2)}, u32[]{:S(2)}) collective-permute-start(f32[16,1024]{1,0:T(8,128)S(1)} %get-tuple-element.607), channel_id=1, source_target_pairs={{0,1},{1,2},{2,3},{3,4},{4,5},{5,6},{6,7},{7,8},{8,9},{9,10},{10,1... | collective-permute-start | bytes 196616 | tf_op jit(solution)/shard_map/ppermute | solution.py:16
  92.0 1.9 %collective-permute-start = (f32[16,1024]{1,0:T(8,128)S(1)}, f32[16,1024]{1,0:T(8,128)S(1)}, u32[]{:S(2)}, u32[]{:S(2)}) collective-permute-start(f32[16,1024]{1,0:T(8,128)S(1)} %get-tuple-element.326), channel_id=1, source_target_pairs={{0,32},{32,64},{64,96},{96,128},{128,160},{160,192},{192,224},{224... | collective-permute-start | bytes 196616 | tf_op jit(solution)/shard_map/ppermute | solution.py:22
  93.9 1.0 collective-permute-done.5
  95.0 6.2 %collective-permute-done = f32[16,1024]{1,0:T(8,128)S(1)} collective-permute-done((f32[16,1024]{1,0:T(8,128)S(1)}, f32[16,1024]{1,0:T(8,128)S(1)}, u32[]{:S(2)}, u32[]{:S(2)}) %collective-permute-start) | collective-permute-done | bytes 65568 | tf_op jit(solution)/shard_map/ppermute | solution.py:22
  101.2 38.8 %while.61 = (s32[]{:T(128)}, f32[16,1024]{1,0:T(8,128)S(1)}, f32[16,1024]{1,0:T(8,128)S(1)}, f32[16,1024]{1,0:T(8,128)S(1)}, f32[16,1024]{1,0:T(8,128)S(1)}, /*i...) while((s32[]{:T(128)}, f32[16,1024]{1,0:T(8,128)S(1)}, ...), condition=%wide.region_5.6_spmd.clone, body=%wide.region_4.5_spmd.clone.sunk | while | flops 1294402 | bytes 4383153 | solution.py:106
  101.8 0.8 fusion.370
  104.3 0.8 fusion.370
  106.7 0.8 fusion.370
  109.1 0.8 fusion.370
  111.5 0.8 fusion.370
  114.0 0.8 fusion.370
  116.4 0.8 fusion.370
  118.8 0.8 fusion.370
  121.2 0.8 fusion.370
  123.6 0.8 fusion.370
  126.1 0.8 fusion.370
  128.5 0.8 fusion.370
  130.9 0.8 fusion.370
  133.3 0.8 fusion.370
  135.8 0.8 fusion.370
  138.2 0.8 fusion.370
  140.0 2.7 %collective-permute-start.6 = (f32[16,1024]{1,0:T(8,128)S(1)}, f32[16,1024]{1,0:T(8,128)S(1)}, u32[]{:S(2)}, u32[]{:S(2)}) collective-permute-start(f32[16,1024]{1,0:T(8,128)S(1)} %get-tuple-element.333), channel_id=1, source_target_pairs={{1,0},{2,1},{3,2},{4,3},{5,4},{6,5},{7,6},{8,7},{9,8},{10,9},{11,1... | collective-permute-start | bytes 196616 | tf_op jit(solution)/shard_map/ppermute | solution.py:16
  142.6 5.7 %collective-permute-done.6 = f32[16,1024]{1,0:T(8,128)S(1)} collective-permute-done((f32[16,1024]{1,0:T(8,128)S(1)}, f32[16,1024]{1,0:T(8,128)S(1)}, u32[]{:S(2)}, u32[]{:S(2)}) %collective-permute-start.6) | collective-permute-done | bytes 65568 | tf_op jit(solution)/shard_map/ppermute | solution.py:16
  148.4 1.9 %collective-permute-start.7 = (f32[16,1024]{1,0:T(8,128)S(1)}, f32[16,1024]{1,0:T(8,128)S(1)}, u32[]{:S(2)}, u32[]{:S(2)}) collective-permute-start(f32[16,1024]{1,0:T(8,128)S(1)} %add_multiply_fusion), channel_id=1, source_target_pairs={{0,1},{1,2},{2,3},{3,4},{4,5},{5,6},{6,7},{7,8},{8,9},{9,10},{10,1... | collective-permute-start | bytes 196616 | tf_op jit(solution)/shard_map/ppermute | solution.py:16
  150.3 4.2 %collective-permute-done.7 = f32[16,1024]{1,0:T(8,128)S(1)} collective-permute-done((f32[16,1024]{1,0:T(8,128)S(1)}, f32[16,1024]{1,0:T(8,128)S(1)}, u32[]{:S(2)}, u32[]{:S(2)}) %collective-permute-start.7) | collective-permute-done | bytes 65568 | tf_op jit(solution)/shard_map/ppermute | solution.py:16
  154.6 19.2 %while.63 = (s32[]{:T(128)}, f32[16,1024]{1,0:T(8,128)S(1)}, f32[16,1024]{1,0:T(8,128)S(1)}, f32[16,1024]{1,0:T(8,128)S(1)}, f32[16,1024]{1,0:T(8,128)S(1)}, /*i...) while((s32[]{:T(128)}, f32[16,1024]{1,0:T(8,128)S(1)}, ...), condition=%wide.region_7.8_spmd.clone, body=%wide.region_6.7_spmd.clone.sunk | while | flops 1310787 | bytes 4514211 | solution.py:106
  173.8 2.0 %collective-permute-start.8 = (f32[16,1024]{1,0:T(8,128)S(1)}, f32[16,1024]{1,0:T(8,128)S(1)}, u32[]{:S(2)}, u32[]{:S(2)}) collective-permute-start(f32[16,1024]{1,0:T(8,128)S(1)} %get-tuple-element.335), channel_id=1, source_target_pairs={{1,0},{2,1},{3,2},{4,3},{5,4},{6,5},{7,6},{8,7},{9,8},{10,9},{11,1... | collective-permute-start | bytes 196616 | tf_op jit(solution)/shard_map/ppermute | solution.py:16
  175.8 6.2 %collective-permute-done.8 = f32[16,1024]{1,0:T(8,128)S(1)} collective-permute-done((f32[16,1024]{1,0:T(8,128)S(1)}, f32[16,1024]{1,0:T(8,128)S(1)}, u32[]{:S(2)}, u32[]{:S(2)}) %collective-permute-start.8) | collective-permute-done | bytes 65568 | tf_op jit(solution)/shard_map/ppermute | solution.py:16
  (909 shorter events, 94.1 us)
Async XLA Ops:
  0.6 1.4 copy-start.3
  0.7 0.7 copy-start.4
  2.0 2.6 %copy-start = (f32[16,1024]{1,0:T(8,128)S(1)}, f32[16,1024]{1,0:T(8,128)}, u32[]{:S(2)}) copy-start(f32[16,1024]{1,0:T(8,128)} %param.15) | copy-start | bytes 196612
  4.9 0.8 copy-start.1
  4.9 0.9 copy-start.2
  4.9 0.8 copy-start.5
  44.5 10.3 %collective-permute-start.2 = (f32[16,1024]{1,0:T(8,128)S(1)}, f32[16,1024]{1,0:T(8,128)S(1)}, u32[]{:S(2)}, u32[]{:S(2)}) collective-permute-start(f32[16,1024]{1,0:T(8,128)S(1)} %get-tuple-element.328), channel_id=1, source_target_pairs={{1,0},{2,1},{3,2},{4,3},{5,4},{6,5},{7,6},{8,7},{9,8},{10,9},{11,1... | collective-permute-start | bytes 196616 | tf_op jit(solution)/shard_map/ppermute | solution.py:16
  47.2 7.6 %collective-permute-start.1 = (f32[1024]{0:T(1024)S(1)}, f32[1024]{0:T(1024)S(1)}, u32[]{:S(2)}, u32[]{:S(2)}) collective-permute-start(f32[1024]{0:T(1024)S(1)} %bitcast.81), channel_id=1, source_target_pairs={{1,0},{2,1},{3,2},{4,3},{5,4},{6,5},{7,6},{8,7},{9,8},{10,9},{11,1... | collective-permute-start | bytes 12296 | tf_op jit(solution)/shard_map/ppermute | solution.py:16
  54.8 6.2 %collective-permute-start.3 = (f32[16,1024]{1,0:T(8,128)S(1)}, f32[16,1024]{1,0:T(8,128)S(1)}, u32[]{:S(2)}, u32[]{:S(2)}) collective-permute-start(f32[16,1024]{1,0:T(8,128)S(1)} %add_multiply_fusion.2), channel_id=1, source_target_pairs={{0,1},{1,2},{2,3},{3,4},{4,5},{5,6},{6,7},{7,8},{8,9},{9,10},{10,1... | collective-permute-start | bytes 196616 | tf_op jit(solution)/shard_map/ppermute | solution.py:16
  80.5 8.3 %collective-permute-start.4 = (f32[16,1024]{1,0:T(8,128)S(1)}, f32[16,1024]{1,0:T(8,128)S(1)}, u32[]{:S(2)}, u32[]{:S(2)}) collective-permute-start(f32[16,1024]{1,0:T(8,128)S(1)} %get-tuple-element.330), channel_id=1, source_target_pairs={{1,0},{2,1},{3,2},{4,3},{5,4},{6,5},{7,6},{8,7},{9,8},{10,9},{11,1... | collective-permute-start | bytes 196616 | tf_op jit(solution)/shard_map/ppermute | solution.py:16
  88.8 6.2 %collective-permute-start.5 = (f32[16,1024]{1,0:T(8,128)S(1)}, f32[16,1024]{1,0:T(8,128)S(1)}, u32[]{:S(2)}, u32[]{:S(2)}) collective-permute-start(f32[16,1024]{1,0:T(8,128)S(1)} %get-tuple-element.607), channel_id=1, source_target_pairs={{0,1},{1,2},{2,3},{3,4},{4,5},{5,6},{6,7},{7,8},{8,9},{9,10},{10,1... | collective-permute-start | bytes 196616 | tf_op jit(solution)/shard_map/ppermute | solution.py:16
  92.0 9.2 %collective-permute-start = (f32[16,1024]{1,0:T(8,128)S(1)}, f32[16,1024]{1,0:T(8,128)S(1)}, u32[]{:S(2)}, u32[]{:S(2)}) collective-permute-start(f32[16,1024]{1,0:T(8,128)S(1)} %get-tuple-element.326), channel_id=1, source_target_pairs={{0,32},{32,64},{64,96},{96,128},{128,160},{160,192},{192,224},{224... | collective-permute-start | bytes 196616 | tf_op jit(solution)/shard_map/ppermute | solution.py:22
  140.0 8.4 %collective-permute-start.6 = (f32[16,1024]{1,0:T(8,128)S(1)}, f32[16,1024]{1,0:T(8,128)S(1)}, u32[]{:S(2)}, u32[]{:S(2)}) collective-permute-start(f32[16,1024]{1,0:T(8,128)S(1)} %get-tuple-element.333), channel_id=1, source_target_pairs={{1,0},{2,1},{3,2},{4,3},{5,4},{6,5},{7,6},{8,7},{9,8},{10,9},{11,1... | collective-permute-start | bytes 196616 | tf_op jit(solution)/shard_map/ppermute | solution.py:16
  148.4 6.2 %collective-permute-start.7 = (f32[16,1024]{1,0:T(8,128)S(1)}, f32[16,1024]{1,0:T(8,128)S(1)}, u32[]{:S(2)}, u32[]{:S(2)}) collective-permute-start(f32[16,1024]{1,0:T(8,128)S(1)} %add_multiply_fusion), channel_id=1, source_target_pairs={{0,1},{1,2},{2,3},{3,4},{4,5},{5,6},{6,7},{7,8},{8,9},{9,10},{10,1... | collective-permute-start | bytes 196616 | tf_op jit(solution)/shard_map/ppermute | solution.py:16
  173.8 8.3 %collective-permute-start.8 = (f32[16,1024]{1,0:T(8,128)S(1)}, f32[16,1024]{1,0:T(8,128)S(1)}, u32[]{:S(2)}, u32[]{:S(2)}) collective-permute-start(f32[16,1024]{1,0:T(8,128)S(1)} %get-tuple-element.335), channel_id=1, source_target_pairs={{1,0},{2,1},{3,2},{4,3},{5,4},{6,5},{7,6},{8,7},{9,8},{10,9},{11,1... | collective-permute-start | bytes 196616 | tf_op jit(solution)/shard_map/ppermute | solution.py:16
where the time goes:
time: 184 us; the launch traced here: 183 us
  other arithmetic  79 us (43%)
  waiting for transfers between devices  37.6 us (20%)
  local copies, waits for them, and re-layouts  37.2 us (20%)
  starting transfers between devices  22.2 us (12%)
  loops' own time  6.4 us (3%)
    div x512, other arithmetic, advance(): field = total / diag  74.9 us
    ppermute x8, waiting for transfers between devices, passed_along(): return lax.ppermute(array, axis, pairs)  31.4 us
    ppermute x8, starting transfers between devices, passed_along(): return lax.ppermute(array, axis, pairs)  20.3 us
    dynamic_slice x96, local copies, waits for them, and re-layouts, march(): return lax.scan(advance, start, (waves, left_term, right_term))  19.8 us
    dynamic_update_slice x128, local copies, waits for them, and re-layouts, march(): return lax.scan(advance, start, (waves, left_term, right_term))  14.1 us
    another operation x4, loops' own time, march(): return lax.scan(advance, start, (waves, left_term, right_term))  6.4 us
    ppermute x1, waiting for transfers between devices, from_behind(): return lax.ppermute(value, axis, pairs)  6.23 us
  transfers between devices with their start and end apart: 9, of which 8 were waited for; matrix products, arithmetic and copies ran while one was open for 0% of the time, Pallas kernels for 0%

commit v1 on v0

--- a/solution.py
+++ b/solution.py
@@ -1,6 +1,10 @@
+import functools
+
 import jax
 import jax.numpy as jnp
 from jax import lax
+from jax.experimental import pallas as pl
+from jax.experimental.pallas import tpu as pltpu
 from jax.sharding import PartitionSpec as P
 
 JACOBI = 8
@@ -77,33 +81,48 @@
     return ((sigma, kxp, kxm, kyp, kym), left_coef, right_coef, d_dir, d_neu)
 
 
-def march(start, couple, diag, coil, waves, left_term, right_term):
-    sigma, kxp, kxm, kyp, kym = couple
-    cols = jnp.arange(start.shape[-2])[:, None]
-    at_left = (cols == 0).astype(jnp.float32)
-    at_right = (cols == start.shape[-2] - 1).astype(jnp.float32)
+def march_kernel(forced, waves, start, sigma, coil, diag, axp, axm, ayp, aym,
+                 left_term, right_term, end, firsts, lasts):
+    cols_n, rows_n = start.shape
+    cols = lax.broadcasted_iota(jnp.int32, (cols_n, rows_n), 0)
 
-    def advance(previous, inputs):
-        wave, left_val, right_val = inputs
-        rhs = (
-            sigma * previous
-            + coil * wave
-            + at_left * left_val[..., None, :]
-            + at_right * right_val[..., None, :]
-        )
+    def advance(step, previous):
+        rhs = sigma[...] * previous
+        if forced:
+            rhs = rhs + coil[...] * waves[step]
+        left_val = left_term[pl.ds(step, 1), :]
+        right_val = right_term[pl.ds(step, 1), :]
+        rhs = rhs + jnp.where(cols == 0, left_val, 0.0)
+        rhs = rhs + jnp.where(cols == cols_n - 1, right_val, 0.0)
+        base = rhs / diag[...]
         field = previous
         for repeat in range(JACOBI):
-            total = (
-                rhs
-                + kxp * next_column(field)
-                + kxm * prev_column(field)
-                + kyp * next_row(field)
-                + kym * prev_row(field)
+            field = (
+                base
+                + axp[...] * pltpu.roll(field, cols_n - 1, 0)
+                + axm[...] * pltpu.roll(field, 1, 0)
+                + ayp[...] * pltpu.roll(field, rows_n - 1, 1)
+                + aym[...] * pltpu.roll(field, 1, 1)
             )
-            field = total / diag
-        return (field, (field[..., 0, :], field[..., -1, :]))
+        firsts[pl.ds(step, 1), :] = field[0:1, :]
+        lasts[pl.ds(step, 1), :] = field[cols_n - 1:cols_n, :]
+        return field
 
-    return lax.scan(advance, start, (waves, left_term, right_term))
+    end[...] = lax.fori_loop(0, left_term.shape[0], advance, start[...])
+
+
+def march(start, sigma, coil, diag, scaled, waves, left_term, right_term, forced):
+    cols_n, rows_n = start.shape
+    steps = left_term.shape[0]
+    vmem = pl.BlockSpec(memory_space=pltpu.VMEM)
+    field = jax.ShapeDtypeStruct((cols_n, rows_n), jnp.float32)
+    series = jax.ShapeDtypeStruct((steps, rows_n), jnp.float32)
+    return pl.pallas_call(
+        functools.partial(march_kernel, forced),
+        out_shape=(field, series, series),
+        in_specs=[pl.BlockSpec(memory_space=pltpu.SMEM)] + [vmem] * 10,
+        out_specs=(vmem, vmem, vmem),
+    )(waves, start, sigma, coil, diag, *scaled, left_term, right_term)
 
 
 def body(start_states, sigma, labels, nu_table, coil, waveform):
@@ -114,22 +133,28 @@
     first = (place == 0).astype(jnp.float32)
     last = (place == count - 1).astype(jnp.float32)
     couple, left_coef, right_coef, d_dir, d_neu = coefficients(sigma, nu, first, last)
+    ks = couple[1:]
+    scaled_dir = tuple(k / d_dir for k in ks)
+    scaled_neu = tuple(k / d_neu for k in ks)
     zero_waves = jnp.zeros_like(waveform)
     traces = jnp.zeros((waveform.shape[0], states.shape[1]), jnp.float32)
     left_traces = jnp.zeros_like(traces)
     inner_face = 1.0 - last
     ends = states
+    zeros = jnp.zeros_like(states)
     for relax_round in range(SWEEPS):
         if relax_round > 0:
             left_traces = passed_along(traces, "space", 1)
         left_term = left_coef * left_traces
         right_term = right_coef * traces
-        ends, (firsts, lasts) = march(states, couple, d_dir, coil, waveform, left_term, right_term)
+        ends, firsts, lasts = march(
+            states, sigma, coil, d_dir, scaled_dir, waveform, left_term, right_term, True
+        )
         nb_first, nb_coef = passed_along((firsts, left_coef), "space", -1)
         flux = inner_face * (right_coef * (lasts - traces) + nb_coef * (nb_first - traces))
         flux_left = passed_along(flux, "space", 1)
-        unused, (pfirst, plast) = march(
-            jnp.zeros_like(states), couple, d_neu, coil, zero_waves, flux_left, flux
+        unused, pfirst, plast = march(
+            zeros, sigma, coil, d_neu, scaled_neu, zero_waves, flux_left, flux, False
         )
         nb_pfirst = passed_along(pfirst, "space", -1)
         traces = traces + THETA * inner_face * (plast + nb_pfirst)

time: 184 us -> 137 us (0.74)
  the two profiles are of different devices: /device:TPU:120 before, /device:TPU:232 now
where the time goes in v1:
time: 137 us; the launch traced here: 136 us
  Pallas kernels  60 us (44%)
  waiting for transfers between devices  37.3 us (27%)
  starting transfers between devices  22.3 us (16%)
  other arithmetic  11.1 us (8%)
  local copies, waits for them, and re-layouts  4.95 us (4%)
    pallas_call x4, Pallas kernels, march(): pl.pallas_call(functools.partial(march_kernel, forced), out_shape=(field,...  60 us
    ppermute x8, waiting for transfers between devices, passed_along(): return lax.ppermute(array, axis, pairs)  31.4 us
    ppermute x8, starting transfers between devices, passed_along(): return lax.ppermute(array, axis, pairs)  20.4 us
    ppermute x1, waiting for transfers between devices, from_behind(): return lax.ppermute(value, axis, pairs)  5.9 us
    add x1, other arithmetic, reluctivity(): result + jnp.where(labels == material, nu_table[material], jnp.float32(0.0))  3.43 us
  transfers between devices with their start and end apart: 9, of which 8 were waited for; matrix products, arithmetic and copies ran while one was open for 0% of the time, Pallas kernels for 0%

profile of v1, /device:TPU:232, one launch (start us, length us, event | category | flops | bytes accessed | tf_op | source)
XLA Modules:
  0.0 136.5 jit_solution(18195082237613476065)
XLA Ops:
  0.7 0.0 copy-start.8
  0.7 0.6 copy-done.8
  1.3 0.6 fusion.10
  1.9 3.4 %select_add_fusion = f32[16,1024]{1,0:T(8,128)S(1)} fusion(s32[16,1024]{1,0:T(8,128)} %param.8, f32[]{:T(128)} %bitcast.4, f32[]{:T(128)} %bitcast.3, f32[]{:T(128)} %bitcast.2, f32[]{:T(128)} %bitcast.1), kind=kLoop, calls=%fused_computation.19 | loop fusion | flops 180224 | bytes 131088 | tf_op jit(solution)/shard_map/add | solution.py:58
  5.4 0.0 copy-done
  5.4 0.8 multiply_divide_fusion
  6.2 0.8 multiply_divide_fusion.1
  7.0 0.0 copy-done.2
  7.0 0.7 multiply_divide_fusion.5
  7.7 0.0 copy-done.1
  7.7 0.6 mul.218.right_term
  8.3 0.6 mul.216.left_term
  9.0 15.0 %shard_map.77 = (f32[16,1024]{1,0:T(8,128)}, f32[16,1024]{1,0:T(8,128)}, f32[16,1024]{1,0:T(8,128)}) custom-call(f32[16]{0:T(128)} %waves.3, f32[16,1024]{1,0:T(8,128)} %bitcast.19, f32[16,1024]{1,0:T(8,128)} %sigma.7, f32[16,1024]{1,0:T(8,128)} %coil.7, f32[16,1024]{1,0:T(8,128)} %copy-done.1, f32[16,1024]{1,0:T(8,128)} %get-tuple-element.34.axp, ...), custom_call_target="tpu_custom_call" | custom-call | tf_op jit(solution)/shard_map/pallas_call | solution.py:120
  24.0 2.3 %collective-permute-start.2 = (f32[16,1024]{1,0:T(8,128)}, f32[16,1024]{1,0:T(8,128)S(1)}, u32[]{:S(2)}, u32[]{:S(2)}) collective-permute-start(f32[16,1024]{1,0:T(8,128)} %get-tuple-element.14), channel_id=1, source_target_pairs={{1,0},{2,1},{3,2},{4,3},{5,4},{6,5},{7,6},{8,7},{9,8},{10,9},{11,1... | collective-permute-start | bytes 196616 | tf_op jit(solution)/shard_map/ppermute | solution.py:20
  26.3 3.0 %collective-permute-start.1 = (f32[1024]{0:T(1024)S(1)}, f32[1024]{0:T(1024)S(1)}, u32[]{:S(2)}, u32[]{:S(2)}) collective-permute-start(f32[1024]{0:T(1024)S(1)} %bitcast.17), channel_id=1, source_target_pairs={{1,0},{2,1},{3,2},{4,3},{5,4},{6,5},{7,6},{8,7},{9,8},{10,9},{11,1... | collective-permute-start | bytes 12296 | tf_op jit(solution)/shard_map/ppermute | solution.py:20
  29.4 4.6 %collective-permute-done.1 = f32[1024]{0:T(1024)S(1)} collective-permute-done((f32[1024]{0:T(1024)S(1)}, f32[1024]{0:T(1024)S(1)}, u32[]{:S(2)}, u32[]{:S(2)}) %collective-permute-start.1) | collective-permute-done | bytes 4128 | tf_op jit(solution)/shard_map/ppermute | solution.py:20
  33.9 0.0 collective-permute-done.2
  33.9 0.9 add_multiply_fusion.2.right_term
  34.8 0.0 copy-start.3
  34.8 3.5 %collective-permute-start.3 = (f32[16,1024]{1,0:T(8,128)S(1)}, f32[16,1024]{1,0:T(8,128)S(1)}, u32[]{:S(2)}, u32[]{:S(2)}) collective-permute-start(f32[16,1024]{1,0:T(8,128)S(1)} %add_multiply_fusion.2.right_term), channel_id=1, source_target_pairs={{0,1},{1,2},{2,3},{3,4},{4,5},{5,6},{6,7},{7,8},{8,9},{9,10},{10,1... | collective-permute-start | bytes 196616 | tf_op jit(solution)/shard_map/ppermute | solution.py:20
  38.3 2.7 %collective-permute-done.3.left_term = f32[16,1024]{1,0:T(8,128)S(1)} collective-permute-done((f32[16,1024]{1,0:T(8,128)S(1)}, f32[16,1024]{1,0:T(8,128)S(1)}, u32[]{:S(2)}, u32[]{:S(2)}) %collective-permute-start.3) | collective-permute-done | bytes 65568 | tf_op jit(solution)/shard_map/ppermute | solution.py:20
  41.0 0.5 broadcast_7_waves.2.waves
  41.5 0.6 broadcast_in_dim.38.start
  42.1 0.0 copy-done.3
  42.1 0.0 copy-done.7
  42.1 15.0 %shard_map.78 = (f32[16,1024]{1,0:T(8,128)}, f32[16,1024]{1,0:T(8,128)}, f32[16,1024]{1,0:T(8,128)}) custom-call(f32[16]{0:T(128)} %broadcast_7_waves.2.waves, f32[16,1024]{1,0:T(8,128)} %broadcast_in_dim.38.start, f32[16,1024]{1,0:T(8,128)} %sigma.7, f32[16,1024]{1,0:T(8,128)} %coil.7, f32[16,1024]{1,0:T(8,128)} %copy-done.2, ...), custom_call_target="tpu_custom_call" | custom-call | tf_op jit(solution)/shard_map/pallas_call | solution.py:120
  57.1 1.9 %collective-permute-start.4 = (f32[16,1024]{1,0:T(8,128)}, f32[16,1024]{1,0:T(8,128)S(1)}, u32[]{:S(2)}, u32[]{:S(2)}) collective-permute-start(f32[16,1024]{1,0:T(8,128)} %get-tuple-element.16), channel_id=1, source_target_pairs={{1,0},{2,1},{3,2},{4,3},{5,4},{6,5},{7,6},{8,7},{9,8},{10,9},{11,1... | collective-permute-start | bytes 196616 | tf_op jit(solution)/shard_map/ppermute | solution.py:20
  59.0 6.6 %collective-permute-done.4 = f32[16,1024]{1,0:T(8,128)S(1)} collective-permute-done((f32[16,1024]{1,0:T(8,128)}, f32[16,1024]{1,0:T(8,128)S(1)}, u32[]{:S(2)}, u32[]{:S(2)}) %collective-permute-start.4) | collective-permute-done | bytes 65568 | tf_op jit(solution)/shard_map/ppermute | solution.py:20
  65.6 1.5 %broadcast_multiply_fusion = (f32[16,1024]{1,0:T(8,128)}, f32[16,1024]{1,0:T(8,128)S(1)}) fusion(f32[1024]{0:T(1024)S(1)} %bitcast.13, f32[16,1024]{1,0:T(8,128)} %get-tuple-element.15, f32[16,1024]{1,0:T(8,128)S(1)} %collective-permute-done.4, f32[]{:T(128)S(6)} %mul.219), kind=kLoop, calls=%fused_computation.28 | loop fusion | flops 49152 | bytes 266244 | tf_op jit(solution)/shard_map/mul | solution.py:149
  67.1 3.5 %collective-permute-start.5 = (f32[16,1024]{1,0:T(8,128)S(1)}, f32[16,1024]{1,0:T(8,128)S(1)}, u32[]{:S(2)}, u32[]{:S(2)}) collective-permute-start(f32[16,1024]{1,0:T(8,128)S(1)} %get-tuple-element.23), channel_id=1, source_target_pairs={{0,1},{1,2},{2,3},{3,4},{4,5},{5,6},{6,7},{7,8},{8,9},{9,10},{10,1... | collective-permute-start | bytes 196616 | tf_op jit(solution)/shard_map/ppermute | solution.py:20
  70.6 0.0 copy-done.9
  70.6 1.9 %collective-permute-start = (f32[16,1024]{1,0:T(8,128)S(1)}, f32[16,1024]{1,0:T(8,128)S(1)}, u32[]{:S(2)}, u32[]{:S(2)}) collective-permute-start(f32[16,1024]{1,0:T(8,128)S(1)} %copy-done.9), channel_id=1, source_target_pairs={{0,32},{32,64},{64,96},{96,128},{128,160},{160,192},{192,224},{224... | collective-permute-start | bytes 196616 | tf_op jit(solution)/shard_map/ppermute | solution.py:26
  72.5 0.7 collective-permute-done.5
  73.3 0.6 broadcast_multiply_fusion.1.left_term
  73.9 5.9 %collective-permute-done.start = f32[16,1024]{1,0:T(8,128)S(1)} collective-permute-done((f32[16,1024]{1,0:T(8,128)S(1)}, f32[16,1024]{1,0:T(8,128)S(1)}, u32[]{:S(2)}, u32[]{:S(2)}) %collective-permute-start) | collective-permute-done | bytes 65568 | tf_op jit(solution)/shard_map/ppermute | solution.py:26
  79.8 0.6 copy-done.5
  80.4 15.0 %shard_map.79 = (f32[16,1024]{1,0:T(8,128)}, f32[16,1024]{1,0:T(8,128)}, f32[16,1024]{1,0:T(8,128)}) custom-call(f32[16]{0:T(128)} %waves.3, f32[16,1024]{1,0:T(8,128)} %copy-done.5, f32[16,1024]{1,0:T(8,128)} %sigma.7, f32[16,1024]{1,0:T(8,128)} %coil.7, f32[16,1024]{1,0:T(8,128)} %copy-done.1, f32[16,1024]{1,0:T(8,128)} %get-tuple-element.34.axp, ...), custom_call_target="tpu_custom_call" | custom-call | tf_op jit(solution)/shard_map/pallas_call | solution.py:120
  95.4 2.3 %collective-permute-start.6 = (f32[16,1024]{1,0:T(8,128)}, f32[16,1024]{1,0:T(8,128)S(1)}, u32[]{:S(2)}, u32[]{:S(2)}) collective-permute-start(f32[16,1024]{1,0:T(8,128)} %get-tuple-element.19), channel_id=1, source_target_pairs={{1,0},{2,1},{3,2},{4,3},{5,4},{6,5},{7,6},{8,7},{9,8},{10,9},{11,1... | collective-permute-start | bytes 196616 | tf_op jit(solution)/shard_map/ppermute | solution.py:20
  97.8 6.1 %collective-permute-done.6 = f32[16,1024]{1,0:T(8,128)S(1)} collective-permute-done((f32[16,1024]{1,0:T(8,128)}, f32[16,1024]{1,0:T(8,128)S(1)}, u32[]{:S(2)}, u32[]{:S(2)}) %collective-permute-start.6) | collective-permute-done | bytes 65568 | tf_op jit(solution)/shard_map/ppermute | solution.py:20
  103.9 0.9 add_multiply_fusion.right_term
  104.7 0.0 copy-start.4
  104.8 1.9 %collective-permute-start.7 = (f32[16,1024]{1,0:T(8,128)S(1)}, f32[16,1024]{1,0:T(8,128)S(1)}, u32[]{:S(2)}, u32[]{:S(2)}) collective-permute-start(f32[16,1024]{1,0:T(8,128)S(1)} %add_multiply_fusion.right_term), channel_id=1, source_target_pairs={{0,1},{1,2},{2,3},{3,4},{4,5},{5,6},{6,7},{7,8},{8,9},{9,10},{10,1... | collective-permute-start | bytes 196616 | tf_op jit(solution)/shard_map/ppermute | solution.py:20
  106.7 4.2 %collective-permute-done.7.left_term = f32[16,1024]{1,0:T(8,128)S(1)} collective-permute-done((f32[16,1024]{1,0:T(8,128)S(1)}, f32[16,1024]{1,0:T(8,128)S(1)}, u32[]{:S(2)}, u32[]{:S(2)}) %collective-permute-start.7) | collective-permute-done | bytes 65568 | tf_op jit(solution)/shard_map/ppermute | solution.py:20
  110.9 0.6 copy-done.6
  111.5 15.0 %shard_map.80 = (f32[16,1024]{1,0:T(8,128)}, f32[16,1024]{1,0:T(8,128)}, f32[16,1024]{1,0:T(8,128)}) custom-call(f32[16]{0:T(128)} %broadcast_7_waves.2.waves, f32[16,1024]{1,0:T(8,128)} %broadcast_in_dim.38.start, f32[16,1024]{1,0:T(8,128)} %sigma.7, f32[16,1024]{1,0:T(8,128)} %coil.7, f32[16,1024]{1,0:T(8,128)} %copy-done.2, ...), custom_call_target="tpu_custom_call" | custom-call | tf_op jit(solution)/shard_map/pallas_call | solution.py:120
  126.5 1.9 %collective-permute-start.8 = (f32[16,1024]{1,0:T(8,128)}, f32[16,1024]{1,0:T(8,128)S(1)}, u32[]{:S(2)}, u32[]{:S(2)}) collective-permute-start(f32[16,1024]{1,0:T(8,128)} %get-tuple-element.21), channel_id=1, source_target_pairs={{1,0},{2,1},{3,2},{4,3},{5,4},{6,5},{7,6},{8,7},{9,8},{10,9},{11,1... | collective-permute-start | bytes 196616 | tf_op jit(solution)/shard_map/ppermute | solution.py:20
  128.4 6.6 %collective-permute-done.8 = f32[16,1024]{1,0:T(8,128)S(1)} collective-permute-done((f32[16,1024]{1,0:T(8,128)}, f32[16,1024]{1,0:T(8,128)S(1)}, u32[]{:S(2)}, u32[]{:S(2)}) %collective-permute-start.8) | collective-permute-done | bytes 65568 | tf_op jit(solution)/shard_map/ppermute | solution.py:20
  135.0 1.5 %multiply_add_fusion = f32[16,1024]{1,0:T(8,128)} fusion(f32[16,1024]{1,0:T(8,128)S(1)} %get-tuple-element.23, f32[16,1024]{1,0:T(8,128)} %get-tuple-element.20, f32[16,1024]{1,0:T(8,128)S(1)} %collective-permute-done.8, f32[]{:T(128)S(6)} %mul.219), kind=kLoop, calls=%fused_computation.4 | loop fusion | flops 49152 | bytes 262148 | tf_op jit(solution)/shard_map/add | solution.py:160
  (13 shorter events, 0.0 us)
Async XLA Ops:
  0.7 0.7 copy-start.8
  1.9 3.5 %copy-start = (f32[16,1024]{1,0:T(8,128)S(1)}, f32[16,1024]{1,0:T(8,128)}, u32[]{:S(2)}) copy-start(f32[16,1024]{1,0:T(8,128)} %sigma.7) | copy-start | bytes 196612
  6.2 0.8 copy-start.2
  7.0 0.7 copy-start.1
  24.0 10.0 %collective-permute-start.2 = (f32[16,1024]{1,0:T(8,128)}, f32[16,1024]{1,0:T(8,128)S(1)}, u32[]{:S(2)}, u32[]{:S(2)}) collective-permute-start(f32[16,1024]{1,0:T(8,128)} %get-tuple-element.14), channel_id=1, source_target_pairs={{1,0},{2,1},{3,2},{4,3},{5,4},{6,5},{7,6},{8,7},{9,8},{10,9},{11,1... | collective-permute-start | bytes 196616 | tf_op jit(solution)/shard_map/ppermute | solution.py:20
  26.3 7.6 %collective-permute-start.1 = (f32[1024]{0:T(1024)S(1)}, f32[1024]{0:T(1024)S(1)}, u32[]{:S(2)}, u32[]{:S(2)}) collective-permute-start(f32[1024]{0:T(1024)S(1)} %bitcast.17), channel_id=1, source_target_pairs={{1,0},{2,1},{3,2},{4,3},{5,4},{6,5},{7,6},{8,7},{9,8},{10,9},{11,1... | collective-permute-start | bytes 12296 | tf_op jit(solution)/shard_map/ppermute | solution.py:20
  34.8 7.3 %copy-start.3 = (f32[16,1024]{1,0:T(8,128)}, f32[16,1024]{1,0:T(8,128)S(1)}, u32[]{:S(2)}) copy-start(f32[16,1024]{1,0:T(8,128)S(1)} %add_multiply_fusion.2.right_term) | copy-start | bytes 196612
  34.8 6.2 %collective-permute-start.3 = (f32[16,1024]{1,0:T(8,128)S(1)}, f32[16,1024]{1,0:T(8,128)S(1)}, u32[]{:S(2)}, u32[]{:S(2)}) collective-permute-start(f32[16,1024]{1,0:T(8,128)S(1)} %add_multiply_fusion.2.right_term), channel_id=1, source_target_pairs={{0,1},{1,2},{2,3},{3,4},{4,5},{5,6},{6,7},{7,8},{8,9},{9,10},{10,1... | collective-permute-start | bytes 196616 | tf_op jit(solution)/shard_map/ppermute | solution.py:20
  41.0 1.2 copy-start.7
  57.1 8.5 %collective-permute-start.4 = (f32[16,1024]{1,0:T(8,128)}, f32[16,1024]{1,0:T(8,128)S(1)}, u32[]{:S(2)}, u32[]{:S(2)}) collective-permute-start(f32[16,1024]{1,0:T(8,128)} %get-tuple-element.16), channel_id=1, source_target_pairs={{1,0},{2,1},{3,2},{4,3},{5,4},{6,5},{7,6},{8,7},{9,8},{10,9},{11,1... | collective-permute-start | bytes 196616 | tf_op jit(solution)/shard_map/ppermute | solution.py:20
  65.6 5.0 %copy-start.9 = (f32[16,1024]{1,0:T(8,128)S(1)}, f32[16,1024]{1,0:T(8,128)}, u32[]{:S(2)}) copy-start(f32[16,1024]{1,0:T(8,128)} %get-tuple-element.12) | copy-start | bytes 196612
  67.1 6.1 %collective-permute-start.5 = (f32[16,1024]{1,0:T(8,128)S(1)}, f32[16,1024]{1,0:T(8,128)S(1)}, u32[]{:S(2)}, u32[]{:S(2)}) collective-permute-start(f32[16,1024]{1,0:T(8,128)S(1)} %get-tuple-element.23), channel_id=1, source_target_pairs={{0,1},{1,2},{2,3},{3,4},{4,5},{5,6},{6,7},{7,8},{8,9},{9,10},{10,1... | collective-permute-start | bytes 196616 | tf_op jit(solution)/shard_map/ppermute | solution.py:20
  70.6 9.2 %collective-permute-start = (f32[16,1024]{1,0:T(8,128)S(1)}, f32[16,1024]{1,0:T(8,128)S(1)}, u32[]{:S(2)}, u32[]{:S(2)}) collective-permute-start(f32[16,1024]{1,0:T(8,128)S(1)} %copy-done.9), channel_id=1, source_target_pairs={{0,32},{32,64},{64,96},{96,128},{128,160},{160,192},{192,224},{224... | collective-permute-start | bytes 196616 | tf_op jit(solution)/shard_map/ppermute | solution.py:26
  79.8 0.6 copy-start.5
  95.4 8.5 %collective-permute-start.6 = (f32[16,1024]{1,0:T(8,128)}, f32[16,1024]{1,0:T(8,128)S(1)}, u32[]{:S(2)}, u32[]{:S(2)}) collective-permute-start(f32[16,1024]{1,0:T(8,128)} %get-tuple-element.19), channel_id=1, source_target_pairs={{1,0},{2,1},{3,2},{4,3},{5,4},{6,5},{7,6},{8,7},{9,8},{10,9},{11,1... | collective-permute-start | bytes 196616 | tf_op jit(solution)/shard_map/ppermute | solution.py:20
  104.7 6.2 %copy-start.4 = (f32[16,1024]{1,0:T(8,128)}, f32[16,1024]{1,0:T(8,128)S(1)}, u32[]{:S(2)}) copy-start(f32[16,1024]{1,0:T(8,128)S(1)} %add_multiply_fusion.right_term) | copy-start | bytes 196612
  104.8 6.2 %collective-permute-start.7 = (f32[16,1024]{1,0:T(8,128)S(1)}, f32[16,1024]{1,0:T(8,128)S(1)}, u32[]{:S(2)}, u32[]{:S(2)}) collective-permute-start(f32[16,1024]{1,0:T(8,128)S(1)} %add_multiply_fusion.right_term), channel_id=1, source_target_pairs={{0,1},{1,2},{2,3},{3,4},{4,5},{5,6},{6,7},{7,8},{8,9},{9,10},{10,1... | collective-permute-start | bytes 196616 | tf_op jit(solution)/shard_map/ppermute | solution.py:20
  110.9 0.6 copy-start.6
  126.5 8.5 %collective-permute-start.8 = (f32[16,1024]{1,0:T(8,128)}, f32[16,1024]{1,0:T(8,128)S(1)}, u32[]{:S(2)}, u32[]{:S(2)}) collective-permute-start(f32[16,1024]{1,0:T(8,128)} %get-tuple-element.21), channel_id=1, source_target_pairs={{1,0},{2,1},{3,2},{4,3},{5,4},{6,5},{7,6},{8,7},{9,8},{10,9},{11,1... | collective-permute-start | bytes 196616 | tf_op jit(solution)/shard_map/ppermute | solution.py:20

commit v2 on v1

--- a/solution.py
+++ b/solution.py
@@ -81,10 +81,14 @@
     return ((sigma, kxp, kxm, kyp, kym), left_coef, right_coef, d_dir, d_neu)
 
 
-def march_kernel(forced, waves, start, sigma, coil, diag, axp, axm, ayp, aym,
-                 left_term, right_term, end, firsts, lasts):
+MESH = pl.DeviceIdType.MESH
+
+
+def march_steps(waves, sigma, coil, diag, scaled, start, left_term, right_term,
+                end, firsts, lasts, forced):
     cols_n, rows_n = start.shape
     cols = lax.broadcasted_iota(jnp.int32, (cols_n, rows_n), 0)
+    axp, axm, ayp, aym = scaled
 
     def advance(step, previous):
         rhs = sigma[...] * previous
@@ -108,21 +112,144 @@
         lasts[pl.ds(step, 1), :] = field[cols_n - 1:cols_n, :]
         return field
 
-    end[...] = lax.fori_loop(0, left_term.shape[0], advance, start[...])
-
-
-def march(start, sigma, coil, diag, scaled, waves, left_term, right_term, forced):
-    cols_n, rows_n = start.shape
-    steps = left_term.shape[0]
+    end[...] = lax.fori_loop(0, left_term.shape[0], advance, start)
+
+
+def relax_kernel(waves, states, sigma, coil, nu, d_dir, d_neu,
+                 axp_d, axm_d, ayp_d, aym_d, axp_n, axm_n, ayp_n, aym_n,
+                 ends, traces,
+                 sent_first, lasts, flux, pfirst, plast, ends0, left_term, right_term,
+                 got_first, flux_left, got_pfirst, left_traces, got_state,
+                 send_sem, recv_sem):
+    cols_n, rows_n = states.shape
+    steps = traces.shape[0]
+    n_space = lax.axis_size("space")
+    n_tm = lax.axis_size("tm")
+    me_s = lax.axis_index("space")
+    me_t = lax.axis_index("tm")
+    has_left = me_s > 0
+    has_right = me_s < n_space - 1
+    left = (me_t, lax.rem(me_s + n_space - 1, n_space))
+    right = (me_t, lax.rem(me_s + 1, n_space))
+    tm_next = (lax.rem(me_t + 1, n_tm), me_s)
+    tm_prev = (lax.rem(me_t + n_tm - 1, n_tm), me_s)
+
+    barrier = pltpu.get_barrier_semaphore()
+
+    @pl.when(has_left)
+    def _():
+        pl.semaphore_signal(barrier, inc=1, device_id=left, device_id_type=MESH)
+
+    @pl.when(has_right)
+    def _():
+        pl.semaphore_signal(barrier, inc=1, device_id=right, device_id_type=MESH)
+
+    pl.semaphore_signal(barrier, inc=1, device_id=tm_next, device_id_type=MESH)
+    pl.semaphore_signal(barrier, inc=1, device_id=tm_prev, device_id_type=MESH)
+    pl.semaphore_wait(barrier, 2 + has_left.astype(jnp.int32) + has_right.astype(jnp.int32))
+
+    left_coef = 2.0 * nu[0:1, :]
+    right_coef = 2.0 * nu[cols_n - 1:cols_n, :]
+    inner_face = jnp.where(has_right, 1.0, 0.0).astype(jnp.float32)
+
+    def send(slot, src, dst, target, sends):
+        copy = pltpu.make_async_remote_copy(
+            src_ref=src, dst_ref=dst, send_sem=send_sem.at[slot],
+            recv_sem=recv_sem.at[slot], device_id=target, device_id_type=MESH,
+        )
+
+        @pl.when(sends)
+        def _():
+            copy.start()
+
+        return copy
+
+    def finish(copy, sends, receives, dst):
+        @pl.when(sends)
+        def _():
+            copy.wait_send()
+
+        @pl.when(receives)
+        def _():
+            copy.wait_recv()
+
+        @pl.when(jnp.logical_not(receives))
+        def _():
+            dst[...] = jnp.zeros(dst.shape, dst.dtype)
+
+    traces[...] = jnp.zeros(traces.shape, jnp.float32)
+    start = states[...]
+    scaled_dir = (axp_d, axm_d, ayp_d, aym_d)
+    scaled_neu = (axp_n, axm_n, ayp_n, aym_n)
+    state_copy = None
+    for sweep in range(SWEEPS):
+        base = 5 * sweep
+        if sweep > 0:
+            copy = send(base + 0, traces, left_traces.at[sweep], right, has_right)
+            finish(copy, has_right, has_left, left_traces.at[sweep])
+            left_term[...] = left_coef * left_traces[sweep]
+            state_copy.wait_send()
+            state_copy.wait_recv()
+            start = got_state[...]
+        else:
+            left_term[...] = jnp.zeros(left_term.shape, jnp.float32)
+        right_term[...] = right_coef * traces[...]
+        end = ends if sweep + 1 == SWEEPS else ends0
+        march_steps(waves, sigma, coil, d_dir, scaled_dir, start, left_term, right_term,
+                    end, sent_first.at[sweep, pl.ds(0, steps)], lasts, True)
+        if sweep + 1 < SWEEPS:
+            state_copy = send(base + 4, ends0, got_state, tm_next, True)
+        sent_first[sweep, pl.ds(steps, 8), :] = jnp.broadcast_to(left_coef, (8, rows_n))
+        copy = send(base + 1, sent_first.at[sweep], got_first.at[sweep], left, has_left)
+        finish(copy, has_left, has_right, got_first.at[sweep])
+        nb_first = got_first[sweep, pl.ds(0, steps), :]
+        nb_coef = got_first[sweep, pl.ds(steps, 1), :]
+        g = traces[...]
+        flux[sweep] = inner_face * (right_coef * (lasts[...] - g) + nb_coef * (nb_first - g))
+        copy = send(base + 2, flux.at[sweep], flux_left.at[sweep], right, has_right)
+        finish(copy, has_right, has_left, flux_left.at[sweep])
+        march_steps(waves, sigma, coil, d_neu, scaled_neu,
+                    jnp.zeros((cols_n, rows_n), jnp.float32),
+                    flux_left.at[sweep], flux.at[sweep],
+                    ends0 if sweep + 1 == SWEEPS else left_term,
+                    pfirst.at[sweep], plast, False)
+        copy = send(base + 3, pfirst.at[sweep], got_pfirst.at[sweep], left, has_left)
+        finish(copy, has_left, has_right, got_pfirst.at[sweep])
+        traces[...] = traces[...] + THETA * inner_face * (plast[...] + got_pfirst[sweep])
+
+
+def relax(waveform, states, sigma, coil, nu, d_dir, d_neu, scaled_dir, scaled_neu):
+    cols_n, rows_n = states.shape
+    steps = waveform.shape[0]
     vmem = pl.BlockSpec(memory_space=pltpu.VMEM)
     field = jax.ShapeDtypeStruct((cols_n, rows_n), jnp.float32)
     series = jax.ShapeDtypeStruct((steps, rows_n), jnp.float32)
+    plane = pltpu.VMEM((steps, rows_n), jnp.float32)
+    pair = pltpu.VMEM((SWEEPS, steps, rows_n), jnp.float32)
     return pl.pallas_call(
-        functools.partial(march_kernel, forced),
-        out_shape=(field, series, series),
-        in_specs=[pl.BlockSpec(memory_space=pltpu.SMEM)] + [vmem] * 10,
-        out_specs=(vmem, vmem, vmem),
-    )(waves, start, sigma, coil, diag, *scaled, left_term, right_term)
+        relax_kernel,
+        out_shape=(field, series),
+        in_specs=[pl.BlockSpec(memory_space=pltpu.SMEM)] + [vmem] * 14,
+        out_specs=(vmem, vmem),
+        scratch_shapes=[
+            pltpu.VMEM((SWEEPS, steps + 8, rows_n), jnp.float32),
+            plane,
+            pair,
+            pair,
+            plane,
+            pltpu.VMEM((cols_n, rows_n), jnp.float32),
+            pltpu.VMEM((cols_n, rows_n), jnp.float32),
+            plane,
+            pltpu.VMEM((SWEEPS, steps + 8, rows_n), jnp.float32),
+            pair,
+            pair,
+            pair,
+            pltpu.VMEM((cols_n, rows_n), jnp.float32),
+            pltpu.SemaphoreType.DMA((5 * SWEEPS,)),
+            pltpu.SemaphoreType.DMA((5 * SWEEPS,)),
+        ],
+        compiler_params=pltpu.CompilerParams(collective_id=0, has_side_effects=True),
+    )(waveform, states, sigma, coil, nu, d_dir, d_neu, *scaled_dir, *scaled_neu)
 
 
 def body(start_states, sigma, labels, nu_table, coil, waveform):
@@ -136,30 +263,7 @@
     ks = couple[1:]
     scaled_dir = tuple(k / d_dir for k in ks)
     scaled_neu = tuple(k / d_neu for k in ks)
-    zero_waves = jnp.zeros_like(waveform)
-    traces = jnp.zeros((waveform.shape[0], states.shape[1]), jnp.float32)
-    left_traces = jnp.zeros_like(traces)
-    inner_face = 1.0 - last
-    ends = states
-    zeros = jnp.zeros_like(states)
-    for relax_round in range(SWEEPS):
-        if relax_round > 0:
-            left_traces = passed_along(traces, "space", 1)
-        left_term = left_coef * left_traces
-        right_term = right_coef * traces
-        ends, firsts, lasts = march(
-            states, sigma, coil, d_dir, scaled_dir, waveform, left_term, right_term, True
-        )
-        nb_first, nb_coef = passed_along((firsts, left_coef), "space", -1)
-        flux = inner_face * (right_coef * (lasts - traces) + nb_coef * (nb_first - traces))
-        flux_left = passed_along(flux, "space", 1)
-        unused, pfirst, plast = march(
-            zeros, sigma, coil, d_neu, scaled_neu, zero_waves, flux_left, flux, False
-        )
-        nb_pfirst = passed_along(pfirst, "space", -1)
-        traces = traces + THETA * inner_face * (plast + nb_pfirst)
-        if relax_round + 1 < SWEEPS:
-            states = from_behind(ends, "tm", 1)
+    ends, traces = relax(waveform, states, sigma, coil, nu, d_dir, d_neu, scaled_dir, scaled_neu)
     return (ends[None], traces)
 
 

time: 137 us -> 103 us (0.75)
  waiting for transfers between devices: 37.3 us -> 0 us
  Pallas kernels: 60 us -> 92.4 us
  starting transfers between devices: 22.3 us -> 0 us
  other arithmetic: 11.1 us -> 5.69 us
  local copies, waits for them, and re-layouts: 4.95 us -> 3.42 us
    ppermute x9 -> x0, waiting for transfers between devices: 37.3 us -> none  [the longest x8 31.4 us: passed_along(): return lax.ppermute(array, axis, pairs)]
    pallas_call x4 -> x1, Pallas kernels: 60 us -> 92.4 us  [relax(): pl.pallas_call(relax_kernel, out_shape=(field, series), in_specs=[pl.Bloc...]
    ppermute x9 -> x0, starting transfers between devices: 22.3 us -> none  [the longest x8 20.4 us: passed_along(): return lax.ppermute(array, axis, pairs)]
    mul x6 -> x0, other arithmetic: 3.86 us -> none  [the longest x2 1.72 us: body(): inner_face * (right_coef * (lasts - traces) + nb_coef * (nb_first - traces))]
    add x1 -> x0, other arithmetic: 1.48 us -> none  [body(): traces = traces + THETA * inner_face * (plast + nb_pfirst)]
    unnamed x20 -> x14, local copies, waits for them, and re-layouts: 1.91 us -> 2.81 us
  transfers between devices with their start and end apart: 9 -> 0, of which waited for: 8 -> 0; matrix products, arithmetic and copies ran while one was open for 0% -> 0% of each run, Pallas kernels for 0% -> 0%
where the time goes in v2:
time: 103 us; the launch traced here: 102 us
  Pallas kernels  92.4 us (90%)
  other arithmetic  5.69 us (6%)
  local copies, waits for them, and re-layouts  3.42 us (3%)
    pallas_call x1, Pallas kernels, relax(): pl.pallas_call(relax_kernel, out_shape=(field, series), in_specs=[pl.Bloc...  92.4 us
    add x1, other arithmetic, reluctivity(): result + jnp.where(labels == material, nu_table[material], jnp.float32(0.0))  3.39 us
    unnamed x14, local copies, waits for them, and re-layouts  2.81 us

profile of v2, /device:TPU:232, one launch (start us, length us, event | category | flops | bytes accessed | tf_op | source)
XLA Modules:
  0.0 102.2 jit_solution(1753975607891912457)
XLA Ops:
  0.7 0.0 copy-start.5
  0.7 0.6 copy-done.5
  1.3 0.6 fusion.10
  1.9 0.0 copy-start.3
  1.9 3.4 %select_add_fusion.nu = f32[16,1024]{1,0:T(8,128)S(1)} fusion(s32[16,1024]{1,0:T(8,128)} %param.8, f32[]{:T(128)} %bitcast.4, f32[]{:T(128)} %bitcast.3, f32[]{:T(128)} %bitcast.2, f32[]{:T(128)} %bitcast.1), kind=kLoop, calls=%fused_computation.15 | loop fusion | flops 180224 | bytes 131088 | tf_op jit(solution)/shard_map/add | solution.py:58
  5.3 0.0 copy-start
  5.4 0.0 copy-done.3
  5.4 0.8 multiply_divide_fusion
  6.1 0.0 copy-start.2
  6.1 0.8 multiply_divide_fusion.1
  6.9 0.0 copy-done.2
  6.9 0.0 copy-start.1
  6.9 0.0 copy-done
  6.9 0.7 multiply_divide_fusion.5
  7.7 0.0 copy-done.1
  7.7 92.4 %shard_map.77 = (f32[16,1024]{1,0:T(8,128)}, f32[16,1024]{1,0:T(8,128)}) custom-call(f32[16]{0:T(128)} %waves.1, f32[16,1024]{1,0:T(8,128)} %bitcast.10, f32[16,1024]{1,0:T(8,128)} %sigma.1, f32[16,1024]{1,0:T(8,128)} %coil.1, f32[16,1024]{1,0:T(8,128)} %copy-done, f32[16,1024]{1,0:T(8,128)} %copy-done.1, f32[16,1024]{1,0:T(8,128)} %copy-done.2, ...), custom_call_target="tpu_custom_call" | custom-call | tf_op jit(solution)/shard_map/pallas_call | solution.py:229
  100.0 0.0 copy-start.4
  100.0 1.5 %copy.10 = f32[1,16,1024]{2,1,0:T(8,128)} copy(f32[1,16,1024]{2,1,0:T(8,128)} %bitcast.11) | data formatting | bytes 131072
  101.6 0.0 copy-done.4
  101.6 0.6 copy.11
  (3 shorter events, 0.0 us)
Async XLA Ops:
  0.7 0.7 copy-start.5
  1.9 3.4 %copy-start.3 = (f32[16,1024]{1,0:T(8,128)S(1)}, f32[16,1024]{1,0:T(8,128)}, u32[]{:S(2)}) copy-start(f32[16,1024]{1,0:T(8,128)} %sigma.1) | copy-start | bytes 196612
  5.3 1.6 %copy-start = (f32[16,1024]{1,0:T(8,128)}, f32[16,1024]{1,0:T(8,128)S(1)}, u32[]{:S(2)}) copy-start(f32[16,1024]{1,0:T(8,128)S(1)} %select_add_fusion.nu) | copy-start | bytes 196612
  6.1 0.8 copy-start.2
  6.9 0.7 copy-start.1
  100.0 1.5 %copy-start.4 = (f32[16,1024]{1,0:T(8,128)S(1)}, f32[16,1024]{1,0:T(8,128)}, u32[]{:S(2)}) copy-start(f32[16,1024]{1,0:T(8,128)} %get-tuple-element.32) | copy-start | bytes 196612

commit v3 on v2

--- a/solution.py
+++ b/solution.py
@@ -86,30 +86,39 @@
 
 def march_steps(waves, sigma, coil, diag, scaled, start, left_term, right_term,
                 end, firsts, lasts, forced):
-    cols_n, rows_n = start.shape
-    cols = lax.broadcasted_iota(jnp.int32, (cols_n, rows_n), 0)
+    cols_n, subs, lanes = start.shape
+    lane = lax.broadcasted_iota(jnp.int32, (1, subs, lanes), 2)
+    at_first = lane == 0
+    at_last = lane == lanes - 1
     axp, axm, ayp, aym = scaled
 
     def advance(step, previous):
         rhs = sigma[...] * previous
         if forced:
             rhs = rhs + coil[...] * waves[step]
-        left_val = left_term[pl.ds(step, 1), :]
-        right_val = right_term[pl.ds(step, 1), :]
-        rhs = rhs + jnp.where(cols == 0, left_val, 0.0)
-        rhs = rhs + jnp.where(cols == cols_n - 1, right_val, 0.0)
+        left_val = left_term[pl.ds(step, 1)]
+        right_val = right_term[pl.ds(step, 1)]
+        rhs = jnp.concatenate(
+            [rhs[0:1] + left_val, rhs[1:cols_n - 1], rhs[cols_n - 1:] + right_val], axis=0
+        )
         base = rhs / diag[...]
         field = previous
         for repeat in range(JACOBI):
+            up = pltpu.roll(field, lanes - 1, 2)
+            up = jnp.where(at_last, pltpu.roll(up, subs - 1, 1), up)
+            down = pltpu.roll(field, 1, 2)
+            down = jnp.where(at_first, pltpu.roll(down, 1, 1), down)
+            east = jnp.concatenate([field[1:], field[:1]], axis=0)
+            west = jnp.concatenate([field[cols_n - 1:], field[:cols_n - 1]], axis=0)
             field = (
                 base
-                + axp[...] * pltpu.roll(field, cols_n - 1, 0)
-                + axm[...] * pltpu.roll(field, 1, 0)
-                + ayp[...] * pltpu.roll(field, rows_n - 1, 1)
-                + aym[...] * pltpu.roll(field, 1, 1)
+                + axp[...] * east
+                + axm[...] * west
+                + ayp[...] * up
+                + aym[...] * down
             )
-        firsts[pl.ds(step, 1), :] = field[0:1, :]
-        lasts[pl.ds(step, 1), :] = field[cols_n - 1:cols_n, :]
+        firsts[pl.ds(step, 1)] = field[0:1]
+        lasts[pl.ds(step, 1)] = field[cols_n - 1:]
         return field
 
     end[...] = lax.fori_loop(0, left_term.shape[0], advance, start)
@@ -121,7 +130,7 @@
                  sent_first, lasts, flux, pfirst, plast, ends0, left_term, right_term,
                  got_first, flux_left, got_pfirst, left_traces, got_state,
                  send_sem, recv_sem):
-    cols_n, rows_n = states.shape
+    cols_n, subs, lanes = states.shape
     steps = traces.shape[0]
     n_space = lax.axis_size("space")
     n_tm = lax.axis_size("tm")
@@ -148,8 +157,8 @@
     pl.semaphore_signal(barrier, inc=1, device_id=tm_prev, device_id_type=MESH)
     pl.semaphore_wait(barrier, 2 + has_left.astype(jnp.int32) + has_right.astype(jnp.int32))
 
-    left_coef = 2.0 * nu[0:1, :]
-    right_coef = 2.0 * nu[cols_n - 1:cols_n, :]
+    left_coef = 2.0 * nu[0:1]
+    right_coef = 2.0 * nu[cols_n - 1:]
     inner_face = jnp.where(has_right, 1.0, 0.0).astype(jnp.float32)
 
     def send(slot, src, dst, target, sends):
@@ -199,17 +208,17 @@
                     end, sent_first.at[sweep, pl.ds(0, steps)], lasts, True)
         if sweep + 1 < SWEEPS:
             state_copy = send(base + 4, ends0, got_state, tm_next, True)
-        sent_first[sweep, pl.ds(steps, 8), :] = jnp.broadcast_to(left_coef, (8, rows_n))
+        sent_first[sweep, pl.ds(steps, 1)] = left_coef
         copy = send(base + 1, sent_first.at[sweep], got_first.at[sweep], left, has_left)
         finish(copy, has_left, has_right, got_first.at[sweep])
-        nb_first = got_first[sweep, pl.ds(0, steps), :]
-        nb_coef = got_first[sweep, pl.ds(steps, 1), :]
+        nb_first = got_first[sweep, pl.ds(0, steps)]
+        nb_coef = got_first[sweep, pl.ds(steps, 1)]
         g = traces[...]
         flux[sweep] = inner_face * (right_coef * (lasts[...] - g) + nb_coef * (nb_first - g))
         copy = send(base + 2, flux.at[sweep], flux_left.at[sweep], right, has_right)
         finish(copy, has_right, has_left, flux_left.at[sweep])
         march_steps(waves, sigma, coil, d_neu, scaled_neu,
-                    jnp.zeros((cols_n, rows_n), jnp.float32),
+                    jnp.zeros((cols_n, subs, lanes), jnp.float32),
                     flux_left.at[sweep], flux.at[sweep],
                     ends0 if sweep + 1 == SWEEPS else left_term,
                     pfirst.at[sweep], plast, False)
@@ -219,32 +228,33 @@
 
 
 def relax(waveform, states, sigma, coil, nu, d_dir, d_neu, scaled_dir, scaled_neu):
-    cols_n, rows_n = states.shape
+    cols_n, subs, lanes = states.shape
     steps = waveform.shape[0]
     vmem = pl.BlockSpec(memory_space=pltpu.VMEM)
-    field = jax.ShapeDtypeStruct((cols_n, rows_n), jnp.float32)
-    series = jax.ShapeDtypeStruct((steps, rows_n), jnp.float32)
-    plane = pltpu.VMEM((steps, rows_n), jnp.float32)
-    pair = pltpu.VMEM((SWEEPS, steps, rows_n), jnp.float32)
+    field = jax.ShapeDtypeStruct((cols_n, subs, lanes), jnp.float32)
+    series = jax.ShapeDtypeStruct((steps, subs, lanes), jnp.float32)
+    plane = pltpu.VMEM((steps, subs, lanes), jnp.float32)
+    pair = pltpu.VMEM((SWEEPS, steps, subs, lanes), jnp.float32)
+    with_coef = pltpu.VMEM((SWEEPS, steps + 1, subs, lanes), jnp.float32)
     return pl.pallas_call(
         relax_kernel,
         out_shape=(field, series),
         in_specs=[pl.BlockSpec(memory_space=pltpu.SMEM)] + [vmem] * 14,
         out_specs=(vmem, vmem),
         scratch_shapes=[
-            pltpu.VMEM((SWEEPS, steps + 8, rows_n), jnp.float32),
+            with_coef,
             plane,
             pair,
             pair,
             plane,
-            pltpu.VMEM((cols_n, rows_n), jnp.float32),
-            pltpu.VMEM((cols_n, rows_n), jnp.float32),
+            pltpu.VMEM((cols_n, subs, lanes), jnp.float32),
+            pltpu.VMEM((cols_n, subs, lanes), jnp.float32),
             plane,
-            pltpu.VMEM((SWEEPS, steps + 8, rows_n), jnp.float32),
-            pair,
-            pair,
-            pair,
-            pltpu.VMEM((cols_n, rows_n), jnp.float32),
+            with_coef,
+            pair,
+            pair,
+            pair,
+            pltpu.VMEM((cols_n, subs, lanes), jnp.float32),
             pltpu.SemaphoreType.DMA((5 * SWEEPS,)),
             pltpu.SemaphoreType.DMA((5 * SWEEPS,)),
         ],
@@ -263,8 +273,14 @@
     ks = couple[1:]
     scaled_dir = tuple(k / d_dir for k in ks)
     scaled_neu = tuple(k / d_neu for k in ks)
-    ends, traces = relax(waveform, states, sigma, coil, nu, d_dir, d_neu, scaled_dir, scaled_neu)
-    return (ends[None], traces)
+    cols_n, rows_n = states.shape
+    lanes = 128
+    tiled = lambda x: x.reshape(x.shape[0], rows_n // lanes, lanes)
+    ends, traces = relax(
+        waveform, tiled(states), tiled(sigma), tiled(coil), tiled(nu), tiled(d_dir), tiled(d_neu),
+        tuple(map(tiled, scaled_dir)), tuple(map(tiled, scaled_neu)),
+    )
+    return (ends.reshape(1, cols_n, rows_n), traces.reshape(traces.shape[0], rows_n))
 
 
 def solution(mesh):

time: 103 us -> 106 us (1.029)
  local copies, waits for them, and re-layouts: 3.42 us -> 13.2 us
  Pallas kernels: 92.4 us -> 85.2 us
    unnamed x14 -> x25, local copies, waits for them, and re-layouts: 2.81 us -> 11.1 us
    pallas_call x1, Pallas kernels: 92.4 us -> 85.2 us  [relax(): pl.pallas_call(relax_kernel, out_shape=(field, series), in_specs=[pl.Bloc...]
    unnamed x0 -> x3, other arithmetic: none -> 2.87 us
    div x3 -> x0, other arithmetic: 2.28 us -> none  [the longest x2 1.54 us: body(): scaled_neu = tuple((k / d_neu for k in ks))]
where the time goes in v3:
time: 106 us; the launch traced here: 105 us
  Pallas kernels  85.2 us (80%)
  local copies, waits for them, and re-layouts  13.2 us (12%)
  other arithmetic  6.34 us (6%)
    pallas_call x1, Pallas kernels, relax(): pl.pallas_call(relax_kernel, out_shape=(field, series), in_specs=[pl.Bloc...  85.2 us
    unnamed x25, local copies, waits for them, and re-layouts  11.1 us
    add x1, other arithmetic, reluctivity(): result + jnp.where(labels == material, nu_table[material], jnp.float32(0.0))  3.45 us
    unnamed x3, other arithmetic  2.87 us

profile of v3, /device:TPU:232, one launch (start us, length us, event | category | flops | bytes accessed | tf_op | source)
XLA Modules:
  0.0 105.5 jit_solution(13034231026733569875)
XLA Ops:
  0.6 1.5 %fusion.12 = (f32[1]{0:T(128)}, f32[1]{0:T(128)}, f32[1]{0:T(128)}, f32[1]{0:T(128)}) fusion(f32[4]{0:T(128)} %param.9), kind=kLoop, calls=%fused_computation.37 | loop fusion | bytes 32 | tf_op jit(solution)/shard_map/slice | solution.py:58
  2.1 0.0 copy-start.1
  2.1 3.4 %select_add_fusion = f32[16,1024]{1,0:T(8,128)S(1)} fusion(s32[16,1024]{1,0:T(8,128)} %param.8, f32[]{:T(128)} %bitcast.3, f32[]{:T(128)} %bitcast.2, f32[]{:T(128)} %bitcast.1, f32[]{:T(128)} %bitcast), kind=kLoop, calls=%fused_computation.16 | loop fusion | flops 180224 | bytes 131088 | tf_op jit(solution)/shard_map/add | solution.py:58
  5.6 0.0 copy-done.1
  5.6 0.1 divide_bitcast_fusion
  5.7 0.2 divide_bitcast_fusion.1
  5.9 0.6 copy.12
  6.6 0.6 copy.13
  7.2 0.6 copy.14
  7.8 0.6 copy.15
  8.5 0.6 copy.16
  9.1 0.6 copy.17
  9.8 0.6 copy.18
  10.4 0.6 copy.19
  11.0 0.6 copy.20
  11.7 0.0 copy-start
  11.7 0.6 copy.21
  12.3 0.2 copy-done
  12.5 2.6 %fusion.13 = f32[2,8,8,128]{3,1,2,0:T(8,128)S(1)} fusion(f32[]{:T(128)} %bitcast.3, s32[16,1024]{1,0:T(8,128)S(1)} %copy-done, f32[]{:T(128)} %bitcast.2, f32[]{:T(128)} %bitcast.1, f32[]{:T(128)} %bitcast), kind=kLoop, calls=%fused_computation.38 | loop fusion | flops 180224 | bytes 131088
  15.1 0.0 copy-start.2
  15.1 0.6 copy.11
  15.7 0.2 copy-done.2
  15.9 0.6 copy.8
  16.6 0.0 copy-start.3
  16.6 0.6 copy.9
  17.2 0.2 copy-done.3
  17.4 0.6 copy.10
  18.1 85.2 %shard_map.77 = (f32[16,8,128]{2,1,0:T(8,128)}, f32[16,8,128]{2,1,0:T(8,128)}) custom-call(f32[16]{0:T(128)} %waves.1, f32[16,8,128]{2,1,0:T(8,128)} %bitcast.63, f32[16,8,128]{2,1,0:T(8,128)} %bitcast.64, f32[16,8,128]{2,1,0:T(8,128)} %bitcast.65, f32[16,8,128]{2,1,0:T(8,128)} %bitcast.62, f32[16,8,128]{2,1,0:T(8,128)} %bitcast.52, f32[16,8,128]{2,1,0:T(8,128)} %bitcast.53, ...), custom_call_target="tpu_custom_call" | custom-call | tf_op jit(solution)/shard_map/pallas_call | solution.py:239
  103.3 0.0 copy-start.4
  103.3 1.5 %copy.24 = f32[2,8,8,128]{3,1,2,0:T(8,128)} copy(f32[2,8,8,128]{3,2,1,0:T(8,128)} %bitcast.69) | data formatting | bytes 131072
  104.8 0.0 copy-done.4
  104.8 0.6 reshape.84
  (3 shorter events, 0.0 us)
Async XLA Ops:
  2.1 3.5 %copy-start.1 = (f32[16,1024]{1,0:T(8,128)S(1)}, f32[16,1024]{1,0:T(8,128)}, u32[]{:S(2)}) copy-start(f32[16,1024]{1,0:T(8,128)} %param.7) | copy-start | bytes 196612
  11.7 0.8 copy-start
  15.1 0.8 copy-start.2
  16.6 0.8 copy-start.3
  103.3 1.5 %copy-start.4 = (f32[16,8,128]{2,1,0:T(8,128)S(1)}, f32[16,8,128]{2,1,0:T(8,128)}, u32[]{:S(2)}) copy-start(f32[16,8,128]{2,1,0:T(8,128)} %get-tuple-element.4) | copy-start | bytes 196612

commit v4 on v3

v4 whole, which is shorter than its diff:
```python
import jax
import jax.numpy as jnp
from jax import lax
from jax.experimental import pallas as pl
from jax.experimental.pallas import tpu as pltpu
from jax.sharding import PartitionSpec as P

JACOBI = 8
SWEEPS = 2
LANES = 128


THETA = 0.25
MESH = pl.DeviceIdType.MESH


def harmonic(first_nu, second_nu):
    return 2.0 * first_nu * second_nu / (first_nu + second_nu)


def row_neighbours(field, at_first, at_last):
    subs, lanes = field.shape[1], field.shape[2]
    up = pltpu.roll(field, lanes - 1, 2)
    up = jnp.where(at_last, pltpu.roll(up, subs - 1, 1), up)
    down = pltpu.roll(field, 1, 2)
    down = jnp.where(at_first, pltpu.roll(down, 1, 1), down)
    return up, down


def march_steps(waves, sigma, coil, diag, scaled, start, left_term, right_term,
                end, firsts, lasts, forced):
    cols_n, subs, lanes = start.shape
    lane = lax.broadcasted_iota(jnp.int32, (1, subs, lanes), 2)
    at_first = lane == 0
    at_last = lane == lanes - 1
    axp, axm, ayp, aym = scaled

    def advance(step, previous):
        rhs = sigma[...] * previous
        if forced:
            rhs = rhs + coil[...] * waves[step]
        left_val = left_term[pl.ds(step, 1)]
        right_val = right_term[pl.ds(step, 1)]
        rhs = jnp.concatenate(
            [rhs[0:1] + left_val, rhs[1:cols_n - 1], rhs[cols_n - 1:] + right_val], axis=0
        )
        base = rhs / diag[...]
        field = previous
        for repeat in range(JACOBI):
            up, down = row_neighbours(field, at_first, at_last)
            east = jnp.concatenate([field[1:], field[:1]], axis=0)
            west = jnp.concatenate([field[cols_n - 1:], field[:cols_n - 1]], axis=0)
            field = (
                base
                + axp[...] * east
                + axm[...] * west
                + ayp[...] * up
                + aym[...] * down
            )
        firsts[pl.ds(step, 1)] = field[0:1]
        lasts[pl.ds(step, 1)] = field[cols_n - 1:]
        return field

    end[...] = lax.fori_loop(0, left_term.shape[0], advance, start)


def relax_kernel(waves, table, packed, ends, traces,
                 coef, sent_first, sent_last, pfirst, plast, ends0, spare,
                 left_term, right_term, g_left, flux_left, flux_right,
                 got_first, got_last, got_pfirst, got_plast, got_state,
                 send_sem, recv_sem):
    _, cols_n, subs, lanes = packed.shape
    steps = traces.shape[0]
    n_space = lax.axis_size("space")
    n_tm = lax.axis_size("tm")
    me_s = lax.axis_index("space")
    me_t = lax.axis_index("tm")
    has_left = me_s > 0
    has_right = me_s < n_space - 1
    left = (me_t, lax.rem(me_s + n_space - 1, n_space))
    right = (me_t, lax.rem(me_s + 1, n_space))
    tm_next = (lax.rem(me_t + 1, n_tm), me_s)
    tm_prev = (lax.rem(me_t + n_tm - 1, n_tm), me_s)

    barrier = pltpu.get_barrier_semaphore()

    @pl.when(has_left)
    def _():
        pl.semaphore_signal(barrier, inc=1, device_id=left, device_id_type=MESH)

    @pl.when(has_right)
    def _():
        pl.semaphore_signal(barrier, inc=1, device_id=right, device_id_type=MESH)

    pl.semaphore_signal(barrier, inc=1, device_id=tm_next, device_id_type=MESH)
    pl.semaphore_signal(barrier, inc=1, device_id=tm_prev, device_id_type=MESH)
    pl.semaphore_wait(barrier, 2 + has_left.astype(jnp.int32) + has_right.astype(jnp.int32))

    sigma = packed.at[1]
    coil = packed.at[2]
    labels = packed[3]
    nu = jnp.zeros(labels.shape, jnp.float32)
    for material in range(table.shape[0]):
        nu = nu + jnp.where(labels == jnp.float32(material), table[material], jnp.float32(0.0))
    lane = lax.broadcasted_iota(jnp.int32, (1, subs, lanes), 2)
    row = lax.broadcasted_iota(jnp.int32, (1, subs, lanes), 1) * lanes + lane
    rows_n = subs * lanes
    up, down = row_neighbours(nu, lane == 0, lane == lanes - 1)
    up = jnp.where(row == rows_n - 1, 0.0, up)
    down = jnp.where(row == 0, 0.0, down)
    blank = jnp.zeros((1, subs, lanes), jnp.float32)
    east = jnp.concatenate([nu[1:], blank], axis=0)
    west = jnp.concatenate([blank, nu[:cols_n - 1]], axis=0)
    kxp = harmonic(nu, east)
    kxm = harmonic(nu, west)
    kyp = harmonic(nu, up)
    kym = harmonic(nu, down)
    edge_rows = jnp.where((row == 0) | (row == rows_n - 1), 1.0, 0.0).astype(jnp.float32)
    inner = sigma[...] + kxp + kxm + kyp + kym + 2.0 * nu * edge_rows
    left_coef = 2.0 * nu[0:1]
    right_coef = 2.0 * nu[cols_n - 1:]
    first_f = jnp.where(has_left, 0.0, 1.0).astype(jnp.float32)
    last_f = jnp.where(has_right, 0.0, 1.0).astype(jnp.float32)
    inner_face = 1.0 - last_f
    d_dir = jnp.concatenate(
        [inner[0:1] + left_coef, inner[1:cols_n - 1], inner[cols_n - 1:] + right_coef], axis=0
    )
    d_neu = jnp.concatenate(
        [inner[0:1] + first_f * left_coef, inner[1:cols_n - 1],
         inner[cols_n - 1:] + last_f * right_coef], axis=0
    )
    coef[0] = d_dir
    coef[1] = d_neu
    for index, k in enumerate((kxp, kxm, kyp, kym)):
        coef[2 + index] = k / d_dir
        coef[6 + index] = k / d_neu
    scaled_dir = tuple(coef.at[2 + index] for index in range(4))
    scaled_neu = tuple(coef.at[6 + index] for index in range(4))

    def send(slot, src, dst, target, sends):
        copy = pltpu.make_async_remote_copy(
            src_ref=src, dst_ref=dst, send_sem=send_sem.at[slot],
            recv_sem=recv_sem.at[slot], device_id=target, device_id_type=MESH,
        )

        @pl.when(sends)
        def _():
            copy.start()

        return copy

    def finish(copy, sends, receives, dst):
        @pl.when(sends)
        def _():
            copy.wait_send()

        @pl.when(receives)
        def _():
            copy.wait_recv()

        @pl.when(jnp.logical_not(receives))
        def _():
            dst[...] = jnp.zeros(dst.shape, dst.dtype)

    traces[...] = jnp.zeros(traces.shape, jnp.float32)
    g_left[...] = jnp.zeros(g_left.shape, jnp.float32)
    start = packed[0]
    state_copy = None
    for sweep in range(SWEEPS):
        base = 5 * sweep
        if sweep > 0:
            left_term[...] = left_coef * g_left[...]
            right_term[...] = right_coef * traces[...]
            state_copy.wait_send()
            state_copy.wait_recv()
            start = got_state[...]
        else:
            left_term[...] = jnp.zeros(left_term.shape, jnp.float32)
            right_term[...] = jnp.zeros(right_term.shape, jnp.float32)
        end = ends if sweep + 1 == SWEEPS else ends0
        march_steps(waves, sigma, coil, coef.at[0], scaled_dir, start, left_term, right_term,
                    end, sent_first.at[sweep, pl.ds(0, steps)],
                    sent_last.at[sweep, pl.ds(0, steps)], True)
        if sweep + 1 < SWEEPS:
            state_copy = send(base + 4, ends0, got_state, tm_next, True)
        sent_first[sweep, pl.ds(steps, 1)] = left_coef
        sent_last[sweep, pl.ds(steps, 1)] = right_coef
        to_left = send(base + 0, sent_first.at[sweep], got_first.at[sweep], left, has_left)
        to_right = send(base + 1, sent_last.at[sweep], got_last.at[sweep], right, has_right)
        finish(to_left, has_left, has_right, got_first.at[sweep])
        finish(to_right, has_right, has_left, got_last.at[sweep])
        g = traces[...]
        lasts = sent_last[sweep, pl.ds(0, steps)]
        nb_first = got_first[sweep, pl.ds(0, steps)]
        nb_coef = got_first[sweep, pl.ds(steps, 1)]
        flux_right[...] = inner_face * (right_coef * (lasts - g) + nb_coef * (nb_first - g))
        gl = g_left[...]
        firsts = sent_first[sweep, pl.ds(0, steps)]
        nb_last = got_last[sweep, pl.ds(0, steps)]
        nb_rcoef = got_last[sweep, pl.ds(steps, 1)]
        from_left = 1.0 * (nb_rcoef * (nb_last - gl) + left_coef * (firsts - gl))
        flux_left[...] = jnp.where(has_left, from_left, 0.0)
        march_steps(waves, sigma, coil, coef.at[1], scaled_neu,
                    jnp.zeros((cols_n, subs, lanes), jnp.float32),
                    flux_left, flux_right,
                    ends0 if sweep + 1 == SWEEPS else spare,
                    pfirst.at[sweep], plast.at[sweep], False)
        to_left = send(base + 2, pfirst.at[sweep], got_pfirst.at[sweep], left, has_left)
        to_right = send(base + 3, plast.at[sweep], got_plast.at[sweep], right, has_right)
        finish(to_left, has_left, has_right, got_pfirst.at[sweep])
        finish(to_right, has_right, has_left, got_plast.at[sweep])
        traces[...] = traces[...] + THETA * inner_face * (plast[sweep] + got_pfirst[sweep])
        gl = g_left[...] + THETA * 1.0 * (got_plast[sweep] + pfirst[sweep])
        g_left[...] = jnp.where(has_left, gl, 0.0)


def relax(waveform, nu_table, packed):
    _, cols_n, subs, lanes = packed.shape
    steps = waveform.shape[0]
    vmem = pl.BlockSpec(memory_space=pltpu.VMEM)
    smem = pl.BlockSpec(memory_space=pltpu.SMEM)
    field = jax.ShapeDtypeStruct((cols_n, subs, lanes), jnp.float32)
    series = jax.ShapeDtypeStruct((steps, subs, lanes), jnp.float32)
    plane = pltpu.VMEM((steps, subs, lanes), jnp.float32)
    whole = pltpu.VMEM((cols_n, subs, lanes), jnp.float32)
    pair = pltpu.VMEM((SWEEPS, steps, subs, lanes), jnp.float32)
    with_coef = pltpu.VMEM((SWEEPS, steps + 1, subs, lanes), jnp.float32)
    return pl.pallas_call(
        relax_kernel,
        out_shape=(field, series),
        in_specs=[smem, smem, vmem],
        out_specs=(vmem, vmem),
        scratch_shapes=[
            pltpu.VMEM((10, cols_n, subs, lanes), jnp.float32),
            with_coef,
            with_coef,
            pair,
            pair,
            whole,
            whole,
            plane,
            plane,
            plane,
            plane,
            plane,
            with_coef,
            with_coef,
            pair,
            pair,
            whole,
            pltpu.SemaphoreType.DMA((5 * SWEEPS,)),
            pltpu.SemaphoreType.DMA((5 * SWEEPS,)),
        ],
        compiler_params=pltpu.CompilerParams(collective_id=0, has_side_effects=True),
    )(waveform, nu_table, packed)


def body(start_states, sigma, labels, nu_table, coil, waveform):
    states = start_states[0]
    cols_n, rows_n = states.shape
    packed = jnp.stack([states, sigma, coil, labels.astype(jnp.float32)])
    packed = packed.reshape(4, cols_n, rows_n // LANES, LANES)
    ends, traces = relax(waveform, nu_table, packed)
    return (ends.reshape(1, cols_n, rows_n), traces.reshape(traces.shape[0], rows_n))


def solution(mesh):
    placed = (
        P("tm", "space", None),
        P("space", None),
        P("space", None),
        P(),
        P("space", None),
        P("tm"),
    )
    return jax.shard_map(
        body,
        mesh=mesh,
        in_specs=placed,
        out_specs=(P("tm", "space", None), P("tm", "space")),
        check_vma=False,
    )
```

time: 106 us -> 78.4 us (0.74)
  the two profiles are of different devices: /device:TPU:232 before, /device:TPU:384 now
where the time goes in v4:
time: 78.4 us; the launch traced here: 78 us
  Pallas kernels  71.9 us (92%)
  local copies, waits for them, and re-layouts  4.72 us (6%)
    pallas_call x1, Pallas kernels, relax(): pl.pallas_call(relax_kernel, out_shape=(field, series), in_specs=[smem, s...  71.9 us
    unnamed x13, local copies, waits for them, and re-layouts  3.21 us

profile of v4, /device:TPU:384, one launch (start us, length us, event | category | flops | bytes accessed | tf_op | source)
XLA Modules:
  0.0 78.0 jit_solution(11574170495670542207)
XLA Ops:
  0.6 0.0 copy-start
  0.6 0.9 %copy.8 = f32[2,8,8,128]{3,2,1,0:T(8,128)S(1)} copy(f32[2,8,8,128]{3,1,2,0:T(8,128)} %bitcast.22) | data formatting | bytes 131072
  1.5 0.0 copy-done
  1.5 0.0 copy-start.1
  1.6 0.8 %copy-done.1 = s32[16,1024]{1,0:T(8,128)S(1)} copy-done((s32[16,1024]{1,0:T(8,128)S(1)}, s32[16,1024]{1,0:T(8,128)}, u32[]{:S(2)}) %copy-start.1) | copy-done | bytes 65560
  2.4 0.0 copy-start.2
  2.4 0.8 %copy-done.2 = f32[16,1024]{1,0:T(8,128)S(1)} copy-done((f32[16,1024]{1,0:T(8,128)S(1)}, f32[16,1024]{1,0:T(8,128)}, u32[]{:S(2)}) %copy-start.2) | copy-done | bytes 65560
  3.2 0.7 pad_maximum_fusion.packed
  4.0 71.9 %shard_map.77 = (f32[16,8,128]{2,1,0:T(8,128)}, f32[16,8,128]{2,1,0:T(8,128)}) custom-call(f32[16]{0:T(128)} %waves.1, f32[4]{0:T(128)} %table.1, f32[4,16,8,128]{3,2,1,0:T(8,128)} %pad_maximum_fusion.packed), custom_call_target="tpu_custom_call" | custom-call | tf_op jit(solution)/shard_map/pallas_call | solution.py:228
  75.9 0.0 copy-start.3
  75.9 1.5 %reshape.18 = f32[1,16,1024]{2,1,0:T(8,128)} reshape(f32[16,8,128]{2,1,0:T(8,128)} %get-tuple-element.4) | data formatting | bytes 131072 | tf_op jit(solution)/shard_map/reshape | solution.py:264
  77.4 0.0 copy-done.3
  77.4 0.6 copy.14
  (4 shorter events, 0.0 us)
Async XLA Ops:
  0.6 0.9 %copy-start = (f32[16,1024]{1,0:T(8,128)S(1)}, f32[16,1024]{1,0:T(8,128)}, u32[]{:S(2)}) copy-start(f32[16,1024]{1,0:T(8,128)} %param.7) | copy-start | bytes 196612
  1.5 0.8 %copy-start.1 = (s32[16,1024]{1,0:T(8,128)S(1)}, s32[16,1024]{1,0:T(8,128)}, u32[]{:S(2)}) copy-start(s32[16,1024]{1,0:T(8,128)} %param.8) | copy-start | bytes 196612
  2.4 0.8 %copy-start.2 = (f32[16,1024]{1,0:T(8,128)S(1)}, f32[16,1024]{1,0:T(8,128)}, u32[]{:S(2)}) copy-start(f32[16,1024]{1,0:T(8,128)} %param.10) | copy-start | bytes 196612
  75.9 1.5 %copy-start.3 = (f32[16,8,128]{2,1,0:T(8,128)S(1)}, f32[16,8,128]{2,1,0:T(8,128)}, u32[]{:S(2)}) copy-start(f32[16,8,128]{2,1,0:T(8,128)} %get-tuple-element.5) | copy-start | bytes 196612

commit v5 on v4

v5 whole, which is shorter than its diff:
```python
import jax
import jax.numpy as jnp
from jax import lax
from jax.experimental import pallas as pl
from jax.experimental.pallas import tpu as pltpu
from jax.sharding import PartitionSpec as P

JACOBI = 8
SWEEPS = 2
LANES = 128


THETA = 0.25
MESH = pl.DeviceIdType.MESH


def harmonic(first_nu, second_nu):
    return 2.0 * first_nu * second_nu / (first_nu + second_nu)


def row_neighbours(field, at_first, at_last):
    subs, lanes = field.shape[1], field.shape[2]
    up = pltpu.roll(field, lanes - 1, 2)
    up = jnp.where(at_last, pltpu.roll(up, subs - 1, 1), up)
    down = pltpu.roll(field, 1, 2)
    down = jnp.where(at_first, pltpu.roll(down, 1, 1), down)
    return up, down


def march_steps(waves, sigma, coil, diag, scaled, start, forced, terms, after, end):
    cols_n, subs, lanes = start.shape
    lane = lax.broadcasted_iota(jnp.int32, (subs, lanes), 1)
    at_first = lane == 0
    at_last = lane == lanes - 1
    axp, axm, ayp, aym = scaled

    def advance(step, previous):
        rhs = sigma[...] * jnp.stack(previous)
        if forced:
            rhs = rhs + coil[...] * waves[step]
        left_val, right_val = terms(step)
        rhs = jnp.concatenate(
            [rhs[0:1] + left_val, rhs[1:cols_n - 1], rhs[cols_n - 1:] + right_val], axis=0
        )
        base = rhs / diag[...]
        field = list(previous)
        for repeat in range(JACOBI):
            fresh = []
            for col in range(cols_n):
                here = field[col]
                up = pltpu.roll(here, lanes - 1, 1)
                up = jnp.where(at_last, pltpu.roll(up, subs - 1, 0), up)
                down = pltpu.roll(here, 1, 1)
                down = jnp.where(at_first, pltpu.roll(down, 1, 0), down)
                across = base[col]
                if col + 1 < cols_n:
                    across = across + axp[col] * field[col + 1]
                if col > 0:
                    across = across + axm[col] * field[col - 1]
                fresh.append(across + (ayp[col] * up + aym[col] * down))
            field = fresh
        after(step, field)
        return tuple(field)

    done = lax.fori_loop(0, waves.shape[0], advance,
                         tuple(start[col] for col in range(cols_n)))
    end[...] = jnp.stack(done)


def relax_kernel(waves, table, packed, ends, traces,
                 coef, sent_first, sent_last, pfirst, plast, ends0, spare, g_left,
                 own_coefs, got_coefs, got_first, got_last, got_pfirst, got_plast, got_state,
                 send_sem, recv_sem):
    _, cols_n, subs, lanes = packed.shape
    steps = traces.shape[0]
    n_space = lax.axis_size("space")
    n_tm = lax.axis_size("tm")
    me_s = lax.axis_index("space")
    me_t = lax.axis_index("tm")
    has_left = me_s > 0
    has_right = me_s < n_space - 1
    no_left = jnp.logical_not(has_left)
    no_right = jnp.logical_not(has_right)
    left = (me_t, lax.rem(me_s + n_space - 1, n_space))
    right = (me_t, lax.rem(me_s + 1, n_space))
    tm_next = (lax.rem(me_t + 1, n_tm), me_s)
    tm_prev = (lax.rem(me_t + n_tm - 1, n_tm), me_s)

    @pl.when(no_right)
    def _():
        got_first[...] = jnp.zeros(got_first.shape, jnp.float32)
        got_pfirst[...] = jnp.zeros(got_pfirst.shape, jnp.float32)
        got_coefs[0] = jnp.zeros(got_coefs.shape[1:], jnp.float32)

    @pl.when(no_left)
    def _():
        got_last[...] = jnp.zeros(got_last.shape, jnp.float32)
        got_plast[...] = jnp.zeros(got_plast.shape, jnp.float32)
        got_coefs[1] = jnp.zeros(got_coefs.shape[1:], jnp.float32)

    barrier = pltpu.get_barrier_semaphore()

    @pl.when(has_left)
    def _():
        pl.semaphore_signal(barrier, inc=1, device_id=left, device_id_type=MESH)

    @pl.when(has_right)
    def _():
        pl.semaphore_signal(barrier, inc=1, device_id=right, device_id_type=MESH)

    pl.semaphore_signal(barrier, inc=1, device_id=tm_next, device_id_type=MESH)
    pl.semaphore_signal(barrier, inc=1, device_id=tm_prev, device_id_type=MESH)
    pl.semaphore_wait(barrier, 2 + has_left.astype(jnp.int32) + has_right.astype(jnp.int32))

    def copy_of(slot, src, dst, target):
        return pltpu.make_async_remote_copy(
            src_ref=src, dst_ref=dst, send_sem=send_sem.at[slot],
            recv_sem=recv_sem.at[slot], device_id=target, device_id_type=MESH,
        )

    def start_if(copy, sends):
        @pl.when(sends)
        def _():
            copy.start()

    def wait_send_if(copy, sends):
        @pl.when(sends)
        def _():
            copy.wait_send()

    def wait_recv_if(copy, receives):
        @pl.when(receives)
        def _():
            copy.wait_recv()

    sigma = packed.at[1]
    coil = packed.at[2]
    labels = packed[3]
    nu = jnp.zeros(labels.shape, jnp.float32)
    for material in range(table.shape[0]):
        nu = nu + jnp.where(labels == jnp.float32(material), table[material], jnp.float32(0.0))
    left_coef = 2.0 * nu[0:1]
    right_coef = 2.0 * nu[cols_n - 1:]
    own_coefs[0] = left_coef[0]
    own_coefs[1] = right_coef[0]
    coef_left = copy_of(0, own_coefs.at[0], got_coefs.at[0], left)
    coef_right = copy_of(1, own_coefs.at[1], got_coefs.at[1], right)
    start_if(coef_left, has_left)
    start_if(coef_right, has_right)

    lane = lax.broadcasted_iota(jnp.int32, (1, subs, lanes), 2)
    row = lax.broadcasted_iota(jnp.int32, (1, subs, lanes), 1) * lanes + lane
    rows_n = subs * lanes
    up, down = row_neighbours(nu, lane == 0, lane == lanes - 1)
    up = jnp.where(row == rows_n - 1, 0.0, up)
    down = jnp.where(row == 0, 0.0, down)
    blank = jnp.zeros((1, subs, lanes), jnp.float32)
    east = jnp.concatenate([nu[1:], blank], axis=0)
    west = jnp.concatenate([blank, nu[:cols_n - 1]], axis=0)
    kxp = harmonic(nu, east)
    kxm = harmonic(nu, west)
    kyp = harmonic(nu, up)
    kym = harmonic(nu, down)
    edge_rows = jnp.where((row == 0) | (row == rows_n - 1), 1.0, 0.0).astype(jnp.float32)
    inner = sigma[...] + kxp + kxm + kyp + kym + 2.0 * nu * edge_rows
    first_f = jnp.where(has_left, 0.0, 1.0).astype(jnp.float32)
    last_f = jnp.where(has_right, 0.0, 1.0).astype(jnp.float32)
    inner_face = 1.0 - last_f
    d_dir = jnp.concatenate(
        [inner[0:1] + left_coef, inner[1:cols_n - 1], inner[cols_n - 1:] + right_coef], axis=0
    )
    d_neu = jnp.concatenate(
        [inner[0:1] + first_f * left_coef, inner[1:cols_n - 1],
         inner[cols_n - 1:] + last_f * right_coef], axis=0
    )
    coef[0] = d_dir
    coef[1] = d_neu
    for index, k in enumerate((kxp, kxm, kyp, kym)):
        coef[2 + index] = k / d_dir
        coef[6 + index] = k / d_neu
    scaled_dir = tuple(coef.at[2 + index] for index in range(4))
    scaled_neu = tuple(coef.at[6 + index] for index in range(4))

    wait_send_if(coef_left, has_left)
    wait_send_if(coef_right, has_right)
    wait_recv_if(coef_left, has_right)
    wait_recv_if(coef_right, has_left)
    nb_coef = got_coefs[0][None]
    nb_rcoef = got_coefs[1][None]

    def row_copies(slot, src, dst, sweep, step):
        to_left = copy_of(slot + step, src[0].at[sweep, pl.ds(step, 1)],
                          dst[0].at[sweep, pl.ds(step, 1)], left)
        to_right = copy_of(slot + steps + step, src[1].at[sweep, pl.ds(step, 1)],
                           dst[1].at[sweep, pl.ds(step, 1)], right)
        return to_left, to_right

    def send_rows(slot, src, dst, sweep, step):
        to_left, to_right = row_copies(slot, src, dst, sweep, step)
        start_if(to_left, has_left)
        start_if(to_right, has_right)

    def settle_rows(slot, src, dst, sweep, step):
        to_left, to_right = row_copies(slot, src, dst, sweep, step)
        wait_send_if(to_left, has_left)
        wait_send_if(to_right, has_right)
        wait_recv_if(to_left, has_right)
        wait_recv_if(to_right, has_left)

    def face_slot(sweep):
        return 3 + 8 * steps * sweep

    def trace_slot(sweep):
        return 3 + 8 * steps * sweep + 4 * steps

    faces = ((sent_first, sent_last), (got_first, got_last))
    neumann = ((pfirst, plast), (got_pfirst, got_plast))

    def update_traces(sweep, step):
        settle_rows(trace_slot(sweep), neumann[0], neumann[1], sweep, step)
        g = traces[pl.ds(step, 1)]
        g = g + THETA * inner_face * (plast[sweep, pl.ds(step, 1)] + got_pfirst[sweep, pl.ds(step, 1)])
        traces[pl.ds(step, 1)] = g
        gl = g_left[pl.ds(step, 1)]
        gl = gl + THETA * 1.0 * (got_plast[sweep, pl.ds(step, 1)] + pfirst[sweep, pl.ds(step, 1)])
        gl = jnp.where(has_left, gl, 0.0)
        g_left[pl.ds(step, 1)] = gl
        return g, gl

    def keeper(slot, rows, sweep):
        def after(step, field):
            rows[0][sweep, pl.ds(step, 1)] = field[0][None]
            rows[1][sweep, pl.ds(step, 1)] = field[cols_n - 1][None]

            @pl.when(step > 0)
            def _():
                send_rows(slot, rows, faces[1] if rows is faces[0] else neumann[1],
                          sweep, step - 1)

        return after

    traces[...] = jnp.zeros(traces.shape, jnp.float32)
    g_left[...] = jnp.zeros(g_left.shape, jnp.float32)
    start = packed[0]
    state_copy = copy_of(2, ends0, got_state, tm_next)
    for sweep in range(SWEEPS):
        if sweep > 0:
            state_copy.wait_send()
            state_copy.wait_recv()
            start = got_state[...]

            def dirichlet_terms(step, sweep=sweep):
                g, gl = update_traces(sweep - 1, step)
                return left_coef * gl, right_coef * g
        else:
            def dirichlet_terms(step):
                return blank, blank
        end = ends if sweep + 1 == SWEEPS else ends0
        march_steps(waves, sigma, coil, coef.at[0], scaled_dir, start, True, dirichlet_terms,
                    keeper(face_slot(sweep), faces[0], sweep), end)
        send_rows(face_slot(sweep), faces[0], faces[1], sweep, steps - 1)
        if sweep + 1 < SWEEPS:
            state_copy.start()

        def neumann_terms(step, sweep=sweep):
            settle_rows(face_slot(sweep), faces[0], faces[1], sweep, step)
            g = traces[pl.ds(step, 1)]
            lasts = sent_last[sweep, pl.ds(step, 1)]
            nb_first = got_first[sweep, pl.ds(step, 1)]
            flux_right = inner_face * (right_coef * (lasts - g) + nb_coef * (nb_first - g))
            gl = g_left[pl.ds(step, 1)]
            firsts = sent_first[sweep, pl.ds(step, 1)]
            nb_last = got_last[sweep, pl.ds(step, 1)]
            from_left = 1.0 * (nb_rcoef * (nb_last - gl) + left_coef * (firsts - gl))
            return jnp.where(has_left, from_left, 0.0), flux_right

        march_steps(waves, sigma, coil, coef.at[1], scaled_neu,
                    jnp.zeros((cols_n, subs, lanes), jnp.float32), False, neumann_terms,
                    keeper(trace_slot(sweep), neumann[0], sweep),
                    ends0 if sweep + 1 == SWEEPS else spare)
        send_rows(trace_slot(sweep), neumann[0], neumann[1], sweep, steps - 1)

    def last_update(step, carry):
        update_traces(SWEEPS - 1, step)
        return carry

    lax.fori_loop(0, steps, last_update, 0)


def relax(waveform, nu_table, packed):
    _, cols_n, subs, lanes = packed.shape
    steps = waveform.shape[0]
    vmem = pl.BlockSpec(memory_space=pltpu.VMEM)
    smem = pl.BlockSpec(memory_space=pltpu.SMEM)
    field = jax.ShapeDtypeStruct((cols_n, subs, lanes), jnp.float32)
    series = jax.ShapeDtypeStruct((steps, subs, lanes), jnp.float32)
    plane = pltpu.VMEM((steps, subs, lanes), jnp.float32)
    whole = pltpu.VMEM((cols_n, subs, lanes), jnp.float32)
    pair = pltpu.VMEM((SWEEPS, steps, subs, lanes), jnp.float32)
    two = pltpu.VMEM((2, subs, lanes), jnp.float32)
    return pl.pallas_call(
        relax_kernel,
        out_shape=(field, series),
        in_specs=[smem, smem, vmem],
        out_specs=(vmem, vmem),
        scratch_shapes=[
            pltpu.VMEM((10, cols_n, subs, lanes), jnp.float32),
            pair,
            pair,
            pair,
            pair,
            whole,
            whole,
            plane,
            two,
            two,
            pair,
            pair,
            pair,
            pair,
            whole,
            pltpu.SemaphoreType.DMA((3 + 8 * steps * SWEEPS,)),
            pltpu.SemaphoreType.DMA((3 + 8 * steps * SWEEPS,)),
        ],
        compiler_params=pltpu.CompilerParams(collective_id=0, has_side_effects=True),
    )(waveform, nu_table, packed)


def body(start_states, sigma, labels, nu_table, coil, waveform):
    states = start_states[0]
    cols_n, rows_n = states.shape
    packed = jnp.stack([states, sigma, coil, labels.astype(jnp.float32)])
    packed = packed.reshape(4, cols_n, rows_n // LANES, LANES)
    ends, traces = relax(waveform, nu_table, packed)
    return (ends.reshape(1, cols_n, rows_n), traces.reshape(traces.shape[0], rows_n))


def solution(mesh):
    placed = (
        P("tm", "space", None),
        P("space", None),
        P("space", None),
        P(),
        P("space", None),
        P("tm"),
    )
    return jax.shard_map(
        body,
        mesh=mesh,
        in_specs=placed,
        out_specs=(P("tm", "space", None), P("tm", "space")),
        check_vma=False,
    )
```

time: 78.4 us -> 65.8 us (0.84)
  the two profiles are of different devices: /device:TPU:384 before, /device:TPU:96 now
where the time goes in v5:
time: 65.8 us; the launch traced here: 65.5 us
  Pallas kernels  59.4 us (90%)
  local copies, waits for them, and re-layouts  4.72 us (7%)
  other arithmetic  0.72 us (1%)
  between operations  0.7 us (1%)
    pallas_call x1, Pallas kernels, relax(): pl.pallas_call(relax_kernel, out_shape=(field, series), in_specs=[smem, s...  59.4 us
    unnamed x13, local copies, waits for them, and re-layouts  3.21 us
    reshape x1, local copies, waits for them, and re-layouts, body(): ends.reshape(1, cols_n, rows_n)  1.52 us

profile of v5, /device:TPU:96, one launch (start us, length us, event | category | flops | bytes accessed | tf_op | source)
XLA Modules:
  0.0 65.5 jit_solution(14487828604932606645)
XLA Ops:
  0.6 0.0 copy-start
  0.6 0.9 %copy.8 = f32[2,8,8,128]{3,2,1,0:T(8,128)S(1)} copy(f32[2,8,8,128]{3,1,2,0:T(8,128)} %bitcast.22) | data formatting | bytes 131072
  1.5 0.0 copy-done
  1.5 0.0 copy-start.1
  1.6 0.8 %copy-done.1 = s32[16,1024]{1,0:T(8,128)S(1)} copy-done((s32[16,1024]{1,0:T(8,128)S(1)}, s32[16,1024]{1,0:T(8,128)}, u32[]{:S(2)}) %copy-start.1) | copy-done | bytes 65560
  2.4 0.0 copy-start.2
  2.4 0.8 %copy-done.2 = f32[16,1024]{1,0:T(8,128)S(1)} copy-done((f32[16,1024]{1,0:T(8,128)S(1)}, f32[16,1024]{1,0:T(8,128)}, u32[]{:S(2)}) %copy-start.2) | copy-done | bytes 65560
  3.2 0.7 %pad_maximum_fusion.packed = f32[4,16,8,128]{3,2,1,0:T(8,128)} fusion(f32[1,16,8,128]{3,2,1,0:T(8,128)S(1)} %bitcast.20, f32[1,16,8,128]{3,2,1,0:T(8,128)S(1)} %bitcast.21, f32[1,16,8,128]{3,2,1,0:T(8,128)S(1)} %bitcast.19, f32[1,16,8,128]{3,2,1,0:T(8,128)S(1)} %bitcast.18), kind=kLoop, calls=%fused_computation | loop fusion | flops 196608 | bytes 524288 | tf_op jit(solution)/shard_map/stack | solution.py:332
  4.0 59.4 %shard_map.77 = (f32[16,8,128]{2,1,0:T(8,128)}, f32[16,8,128]{2,1,0:T(8,128)}) custom-call(f32[16]{0:T(128)} %waves.1, f32[4]{0:T(128)} %table.1, f32[4,16,8,128]{3,2,1,0:T(8,128)} %pad_maximum_fusion.packed), custom_call_target="tpu_custom_call" | custom-call | tf_op jit(solution)/shard_map/pallas_call | solution.py:301
  63.3 0.0 copy-start.3
  63.3 1.5 %reshape.18 = f32[1,16,1024]{2,1,0:T(8,128)} reshape(f32[16,8,128]{2,1,0:T(8,128)} %get-tuple-element.4) | data formatting | bytes 131072 | tf_op jit(solution)/shard_map/reshape | solution.py:335
  64.8 0.0 copy-done.3
  64.8 0.6 copy.14
  (4 shorter events, 0.0 us)
Async XLA Ops:
  0.6 0.9 %copy-start = (f32[16,1024]{1,0:T(8,128)S(1)}, f32[16,1024]{1,0:T(8,128)}, u32[]{:S(2)}) copy-start(f32[16,1024]{1,0:T(8,128)} %param.7) | copy-start | bytes 196612
  1.5 0.8 %copy-start.1 = (s32[16,1024]{1,0:T(8,128)S(1)}, s32[16,1024]{1,0:T(8,128)}, u32[]{:S(2)}) copy-start(s32[16,1024]{1,0:T(8,128)} %param.8) | copy-start | bytes 196612
  2.4 0.8 %copy-start.2 = (f32[16,1024]{1,0:T(8,128)S(1)}, f32[16,1024]{1,0:T(8,128)}, u32[]{:S(2)}) copy-start(f32[16,1024]{1,0:T(8,128)} %param.10) | copy-start | bytes 196612
  63.3 1.5 %copy-start.3 = (f32[16,8,128]{2,1,0:T(8,128)S(1)}, f32[16,8,128]{2,1,0:T(8,128)}, u32[]{:S(2)}) copy-start(f32[16,8,128]{2,1,0:T(8,128)} %get-tuple-element.5) | copy-start | bytes 196612

commit v6 on v5

--- a/solution.py
+++ b/solution.py
@@ -18,20 +18,21 @@
     return 2.0 * first_nu * second_nu / (first_nu + second_nu)
 
 
-def row_neighbours(field, at_first, at_last):
-    subs, lanes = field.shape[1], field.shape[2]
-    up = pltpu.roll(field, lanes - 1, 2)
-    up = jnp.where(at_last, pltpu.roll(up, subs - 1, 1), up)
-    down = pltpu.roll(field, 1, 2)
-    down = jnp.where(at_first, pltpu.roll(down, 1, 1), down)
+def row_neighbours(field, sub):
+    subs, lanes = field.shape[-2], field.shape[-1]
+    ahead = pltpu.roll(field, subs - 1, field.ndim - 2)
+    behind = pltpu.roll(field, 1, field.ndim - 2)
+    edges = jnp.where(sub == 0, behind, ahead)
+    edges = pltpu.roll(edges, 1, field.ndim - 1,
+                       stride=(lanes - 2) // (subs - 1), stride_axis=field.ndim - 2)
+    up = jnp.where(sub == subs - 1, edges, ahead)
+    down = jnp.where(sub == 0, edges, behind)
     return up, down
 
 
 def march_steps(waves, sigma, coil, diag, scaled, start, forced, terms, after, end):
     cols_n, subs, lanes = start.shape
-    lane = lax.broadcasted_iota(jnp.int32, (subs, lanes), 1)
-    at_first = lane == 0
-    at_last = lane == lanes - 1
+    sub = lax.broadcasted_iota(jnp.int32, (subs, lanes), 0)
     axp, axm, ayp, aym = scaled
 
     def advance(step, previous):
@@ -48,10 +49,7 @@
             fresh = []
             for col in range(cols_n):
                 here = field[col]
-                up = pltpu.roll(here, lanes - 1, 1)
-                up = jnp.where(at_last, pltpu.roll(up, subs - 1, 0), up)
-                down = pltpu.roll(here, 1, 1)
-                down = jnp.where(at_first, pltpu.roll(down, 1, 0), down)
+                up, down = row_neighbours(here, sub)
                 across = base[col]
                 if col + 1 < cols_n:
                     across = across + axp[col] * field[col + 1]
@@ -148,10 +146,10 @@
     start_if(coef_left, has_left)
     start_if(coef_right, has_right)
 
-    lane = lax.broadcasted_iota(jnp.int32, (1, subs, lanes), 2)
-    row = lax.broadcasted_iota(jnp.int32, (1, subs, lanes), 1) * lanes + lane
+    sub = lax.broadcasted_iota(jnp.int32, (1, subs, lanes), 1)
+    row = lax.broadcasted_iota(jnp.int32, (1, subs, lanes), 2) * subs + sub
     rows_n = subs * lanes
-    up, down = row_neighbours(nu, lane == 0, lane == lanes - 1)
+    up, down = row_neighbours(nu, sub)
     up = jnp.where(row == rows_n - 1, 0.0, up)
     down = jnp.where(row == 0, 0.0, down)
     blank = jnp.zeros((1, subs, lanes), jnp.float32)
@@ -330,9 +328,12 @@
     states = start_states[0]
     cols_n, rows_n = states.shape
     packed = jnp.stack([states, sigma, coil, labels.astype(jnp.float32)])
-    packed = packed.reshape(4, cols_n, rows_n // LANES, LANES)
+    subs = rows_n // LANES
+    packed = packed.reshape(4, cols_n, LANES, subs).transpose(0, 1, 3, 2)
     ends, traces = relax(waveform, nu_table, packed)
-    return (ends.reshape(1, cols_n, rows_n), traces.reshape(traces.shape[0], rows_n))
+    ends = ends.transpose(0, 2, 1).reshape(1, cols_n, rows_n)
+    traces = traces.transpose(0, 2, 1).reshape(traces.shape[0], rows_n)
+    return (ends, traces)
 
 
 def solution(mesh):

time: 65.8 us -> 69 us (1.049)
  the two profiles are of different devices: /device:TPU:96 before, /device:TPU:224 now
where the time goes in v6:
time: 69 us; the launch traced here: 68.5 us
  Pallas kernels  59.8 us (87%)
  local copies, waits for them, and re-layouts  6.44 us (9%)
  other arithmetic  1.58 us (2%)
  between operations  0.72 us (1%)
    pallas_call x1, Pallas kernels, relax(): pl.pallas_call(relax_kernel, out_shape=(field, series), in_specs=[smem, s...  59.8 us
    unnamed x13, local copies, waits for them, and re-layouts  4.14 us

profile of v6, /device:TPU:224, one launch (start us, length us, event | category | flops | bytes accessed | tf_op | source)
XLA Modules:
  0.0 68.5 jit_solution(16893643530486479761)
XLA Ops:
  0.6 0.8 %convert_element_type.3 = f32[16,1024]{1,0:T(8,128)S(1)} convert(s32[16,1024]{1,0:T(8,128)} %param.8) | non-fusion elementwise | flops 16384 | bytes 131072 | tf_op jit(solution)/shard_map/convert_element_type | solution.py:330
  1.5 0.2 copy.11
  1.7 0.0 copy-start
  1.7 0.2 copy.15
  1.9 0.6 copy-done
  2.5 0.2 copy.8
  2.7 0.0 copy-start.1
  2.7 0.2 copy.12
  2.9 0.6 copy-done.1
  3.6 0.2 copy.9
  3.8 0.0 copy-start.2
  3.8 0.2 copy.13
  4.0 0.6 copy-done.2
  4.6 0.2 copy.10
  4.8 0.2 copy.14
  5.0 0.7 %maximum_bitcast_fusion.packed = f32[4,16,8,128]{3,2,1,0:T(8,128)} fusion(f32[1,16,128,8]{2,3,1,0:T(8,128)S(1)} %copy.15, f32[1,16,128,8]{2,3,1,0:T(8,128)S(1)} %copy.14, f32[1,16,128,8]{2,3,1,0:T(8,128)S(1)} %copy.13, f32[1,16,128,8]{2,3,1,0:T(8,128)S(1)} %copy.12), kind=kLoop, calls=%fused_computation | loop fusion | flops 196608 | bytes 524288 | tf_op jit(solution)/shard_map/transpose | solution.py:332
  5.7 59.8 %shard_map.77 = (f32[16,8,128]{2,1,0:T(8,128)}, f32[16,8,128]{2,1,0:T(8,128)}) custom-call(f32[16]{0:T(128)} %waves.1, f32[4]{0:T(128)} %table.1, f32[4,16,8,128]{3,2,1,0:T(8,128)} %maximum_bitcast_fusion.packed), custom_call_target="tpu_custom_call" | custom-call | tf_op jit(solution)/shard_map/pallas_call | solution.py:299
  65.6 1.1 %copy.17 = f32[16,128,8]{0,2,1:T(8,128)S(1)} copy(f32[16,128,8]{1,2,0:T(8,128)} %bitcast.17) | data formatting | bytes 131072 | tf_op jit(solution)/shard_map/transpose | solution.py:335
  66.7 0.0 copy-start.3
  66.7 0.8 %copy.19 = f32[16,1024]{1,0:T(8,128)} copy(f32[16,1024]{0,1:T(8,128)S(1)} %bitcast.11) | data formatting | bytes 131072
  67.5 0.0 copy-done.3
  67.5 0.2 copy.16
  67.7 0.8 %copy.18 = f32[1,16,1024]{2,1,0:T(8,128)} copy(f32[1,16,1024]{1,2,0:T(8,128)S(1)} %bitcast.12) | data formatting | bytes 131072
Async XLA Ops:
  1.7 0.8 %copy-start = (f32[1,16,1024]{2,1,0:T(8,128)S(1)}, f32[1,16,1024]{2,1,0:T(8,128)}, u32[]{:S(2)}) copy-start(f32[1,16,1024]{2,1,0:T(8,128)} %param.6) | copy-start | bytes 196612
  2.7 0.8 %copy-start.1 = (f32[16,1024]{1,0:T(8,128)S(1)}, f32[16,1024]{1,0:T(8,128)}, u32[]{:S(2)}) copy-start(f32[16,1024]{1,0:T(8,128)} %param.7) | copy-start | bytes 196612
  3.8 0.8 %copy-start.2 = (f32[16,1024]{1,0:T(8,128)S(1)}, f32[16,1024]{1,0:T(8,128)}, u32[]{:S(2)}) copy-start(f32[16,1024]{1,0:T(8,128)} %param.10) | copy-start | bytes 196612
  66.7 0.8 %copy-start.3 = (f32[16,8,128]{2,1,0:T(8,128)S(1)}, f32[16,8,128]{2,1,0:T(8,128)}, u32[]{:S(2)}) copy-start(f32[16,8,128]{2,1,0:T(8,128)} %get-tuple-element.4) | copy-start | bytes 196612

commit v7 on v5

--- a/solution.py
+++ b/solution.py
@@ -67,9 +67,9 @@
     end[...] = jnp.stack(done)
 
 
-def relax_kernel(waves, table, packed, ends, traces,
+def relax_kernel(waves, table, packed, out_ends, out_traces,
                  coef, sent_first, sent_last, pfirst, plast, ends0, spare, g_left,
-                 own_coefs, got_coefs, got_first, got_last, got_pfirst, got_plast, got_state,
+                 own_coefs, got_coefs, got_first, got_last, got_pfirst, got_plast, got_state, ends, traces,
                  send_sem, recv_sem):
     _, cols_n, subs, lanes = packed.shape
     steps = traces.shape[0]
@@ -285,6 +285,11 @@
         return carry
 
     lax.fori_loop(0, steps, last_update, 0)
+    for src, dst in ((ends, out_ends), (traces, out_traces)):
+        for item in range(src.shape[0]):
+            block = src[item]
+            for part in range(subs):
+                dst[pl.ds(item, 1), pl.ds(part * lanes, lanes)] = block[part:part + 1]
 
 
 def relax(waveform, nu_table, packed):
@@ -292,8 +297,8 @@
     steps = waveform.shape[0]
     vmem = pl.BlockSpec(memory_space=pltpu.VMEM)
     smem = pl.BlockSpec(memory_space=pltpu.SMEM)
-    field = jax.ShapeDtypeStruct((cols_n, subs, lanes), jnp.float32)
-    series = jax.ShapeDtypeStruct((steps, subs, lanes), jnp.float32)
+    field = jax.ShapeDtypeStruct((cols_n, subs * lanes), jnp.float32)
+    series = jax.ShapeDtypeStruct((steps, subs * lanes), jnp.float32)
     plane = pltpu.VMEM((steps, subs, lanes), jnp.float32)
     whole = pltpu.VMEM((cols_n, subs, lanes), jnp.float32)
     pair = pltpu.VMEM((SWEEPS, steps, subs, lanes), jnp.float32)
@@ -319,6 +324,8 @@
             pair,
             pair,
             whole,
+            whole,
+            plane,
             pltpu.SemaphoreType.DMA((3 + 8 * steps * SWEEPS,)),
             pltpu.SemaphoreType.DMA((3 + 8 * steps * SWEEPS,)),
         ],
@@ -332,7 +339,7 @@
     packed = jnp.stack([states, sigma, coil, labels.astype(jnp.float32)])
     packed = packed.reshape(4, cols_n, rows_n // LANES, LANES)
     ends, traces = relax(waveform, nu_table, packed)
-    return (ends.reshape(1, cols_n, rows_n), traces.reshape(traces.shape[0], rows_n))
+    return (ends[None], traces)
 
 
 def solution(mesh):

time: 65.8 us -> 65.8 us (level)
    reshape x1 -> x0, local copies, waits for them, and re-layouts: 1.52 us -> none  [body(): ends.reshape(1, cols_n, rows_n)]
    unnamed x13 -> x14, local copies, waits for them, and re-layouts: 3.21 us -> 4.7 us
where the time goes in v7:
time: 65.8 us; the launch traced here: 65.5 us
  Pallas kernels  59.4 us (90%)
  local copies, waits for them, and re-layouts  4.7 us (7%)
  other arithmetic  0.72 us (1%)
  between operations  0.7 us (1%)
    pallas_call x1, Pallas kernels, relax(): pl.pallas_call(relax_kernel, out_shape=(field, series), in_specs=[smem, s...  59.4 us
    unnamed x14, local copies, waits for them, and re-layouts  4.7 us

profile of v7, /device:TPU:96, one launch (start us, length us, event | category | flops | bytes accessed | tf_op | source)
XLA Modules:
  0.0 65.5 jit_solution(3747635412982906323)
XLA Ops:
  0.6 0.0 copy-start
  0.6 0.9 %copy.8 = f32[2,8,8,128]{3,2,1,0:T(8,128)S(1)} copy(f32[2,8,8,128]{3,1,2,0:T(8,128)} %bitcast.19) | data formatting | bytes 131072
  1.5 0.0 copy-done
  1.5 0.0 copy-start.1
  1.6 0.8 %copy-done.1 = s32[16,1024]{1,0:T(8,128)S(1)} copy-done((s32[16,1024]{1,0:T(8,128)S(1)}, s32[16,1024]{1,0:T(8,128)}, u32[]{:S(2)}) %copy-start.1) | copy-done | bytes 65560
  2.4 0.0 copy-start.2
  2.4 0.8 %copy-done.2 = f32[16,1024]{1,0:T(8,128)S(1)} copy-done((f32[16,1024]{1,0:T(8,128)S(1)}, f32[16,1024]{1,0:T(8,128)}, u32[]{:S(2)}) %copy-start.2) | copy-done | bytes 65560
  3.2 0.7 %pad_maximum_fusion.packed = f32[4,16,8,128]{3,2,1,0:T(8,128)} fusion(f32[1,16,8,128]{3,2,1,0:T(8,128)S(1)} %bitcast.17, f32[1,16,8,128]{3,2,1,0:T(8,128)S(1)} %bitcast.18, f32[1,16,8,128]{3,2,1,0:T(8,128)S(1)} %bitcast.16, f32[1,16,8,128]{3,2,1,0:T(8,128)S(1)} %bitcast.15), kind=kLoop, calls=%fused_computation | loop fusion | flops 196608 | bytes 524288 | tf_op jit(solution)/shard_map/stack | solution.py:339
  4.0 59.4 %shard_map.77 = (f32[16,1024]{1,0:T(8,128)}, f32[16,1024]{1,0:T(8,128)}) custom-call(f32[16]{0:T(128)} %waves.1, f32[4]{0:T(128)} %table.1, f32[4,16,8,128]{3,2,1,0:T(8,128)} %pad_maximum_fusion.packed), custom_call_target="tpu_custom_call" | custom-call | tf_op jit(solution)/shard_map/pallas_call | solution.py:306
  63.4 0.0 copy-start.3
  63.4 1.5 %copy.14 = f32[1,16,1024]{2,1,0:T(8,128)} copy(f32[1,16,1024]{2,1,0:T(8,128)} %bitcast.22) | data formatting | bytes 131072
  64.9 0.0 copy-done.3
  64.9 0.6 copy.15
  (4 shorter events, 0.0 us)
Async XLA Ops:
  0.6 0.9 %copy-start = (f32[16,1024]{1,0:T(8,128)S(1)}, f32[16,1024]{1,0:T(8,128)}, u32[]{:S(2)}) copy-start(f32[16,1024]{1,0:T(8,128)} %param.7) | copy-start | bytes 196612
  1.5 0.8 %copy-start.1 = (s32[16,1024]{1,0:T(8,128)S(1)}, s32[16,1024]{1,0:T(8,128)}, u32[]{:S(2)}) copy-start(s32[16,1024]{1,0:T(8,128)} %param.8) | copy-start | bytes 196612
  2.4 0.8 %copy-start.2 = (f32[16,1024]{1,0:T(8,128)S(1)}, f32[16,1024]{1,0:T(8,128)}, u32[]{:S(2)}) copy-start(f32[16,1024]{1,0:T(8,128)} %param.10) | copy-start | bytes 196612
  63.4 1.5 %copy-start.3 = (f32[16,1024]{1,0:T(8,128)S(1)}, f32[16,1024]{1,0:T(8,128)}, u32[]{:S(2)}) copy-start(f32[16,1024]{1,0:T(8,128)} %get-tuple-element.9) | copy-start | bytes 196612
